TPU v7x, 32 devices: a whole 2x2x4 slice. The times are simulated.
32 devices in a mesh: ctx: 8 (over z, y), head: 4 (over x, core).
Axes of the slice: x: 2, y: 2, z: 4, core: 2. Of those that a mesh axis runs over, the one named last changes fastest.
Arguments:
- tokens: bfloat16 [4096, 1024], P('ctx'), may hold values from -24 to 24
- w_query: bfloat16 [1024, 1024], P(None, 'head'), may hold values from -0.1875 to 0.1875
- w_key: bfloat16 [1024, 1024], P(None, 'head'), may hold values from -0.1875 to 0.1875
- w_value: bfloat16 [1024, 1024], P(None, 'head'), may hold values from -0.1875 to 0.1875
- w_out: bfloat16 [1024, 1024], P('head'), may hold values from -0.1875 to 0.1875
- block_mask: int32 [32, 32], replicated, may hold values from 0 to 1, as said below
- block_order: int32 [32], replicated, may hold values from 0 to 31, each once
Outputs:
- mixed: bfloat16 [4096, 1024], P('ctx', 'head')
Inputs may be any that keep to these rules, and one draw needn't show every extreme that they name: `block_mask`: entries are 0 or 1 and every diagonal entry is 1. `block_order`: each initial block index appears once.
All inputs are finite; a program needn't handle non-finite values.
Results may differ from a plain program's by a relative error of at most 0.013.
Values may be sent and summed in bfloat16 or wider, within the bound.
No kernel may reach another device: no remote copies, remote signals or barrier semaphores. Data moves between devices by JAX's collectives and lax.ppermute only.
A program may use at most 256 MiB of HBM per device.

v0:
```python
import functools

import jax
import jax.numpy as jnp
from jax import lax
from jax.experimental import pallas as pl
from jax.experimental.pallas import tpu as pltpu
from jax.sharding import PartitionSpec as P


HEAD_DIM = 64
BLOCK = 128
LANES = 128
SLOTS = 4
STREAMS = 4
NEG = -1e30


HBM = pl.BlockSpec(memory_space=pltpu.HBM)
VMEM = pl.BlockSpec(memory_space=pltpu.VMEM)
SMEM = pl.BlockSpec(memory_space=pltpu.SMEM)
GRANT = 16 * 1024 * 1024
WHOLE = 60 * 1024 * 1024


def low_half(shape):
    return lax.broadcasted_iota(jnp.int32, shape, len(shape) - 1) < HEAD_DIM


def swap_halves(x):
    return pltpu.roll(x, HEAD_DIM, 1)


def proj_kernel(inner, heads, near, tok_in, wk_in, wv_in, wq_in, *rest):
    n_out = 2 * heads - near
    outs, (tok, wk, wv, wq, msg, sems) = rest[:n_out], rest[n_out:]
    loads = [
        pltpu.make_async_copy(src, dst, sems.at[n])
        for n, (src, dst) in enumerate(((tok_in, tok), (wv_in, wv), (wk_in, wk), (wq_in, wq)))
    ]
    for load in loads:
        load.start()
    a = lax.axis_index("ctx") // inner
    rows = tok.shape[0]
    half = rows // 2
    low = low_half((half, LANES))
    loads[0].wait()
    loads[1].wait()
    v = jnp.dot(tok[...], wv[...], preferred_element_type=jnp.float32)
    loads[2].wait()
    loads[3].wait()
    q = jnp.dot(tok[...], wq[...], preferred_element_type=jnp.float32) * HEAD_DIM ** (-0.5)
    k = jnp.dot(tok[...], wk[...], preferred_element_type=jnp.float32)
    for base, x in ((half, v), (rows, q)):
        for g in range(heads // 2):
            for i in range(rows // BLOCK):
                block = x[i * BLOCK : (i + 1) * BLOCK, g * LANES : (g + 1) * LANES]
                turned = jnp.transpose(block).astype(jnp.bfloat16)
                start = base + i * HEAD_DIM
                msg[2 * g, start : start + HEAD_DIM] = turned[:HEAD_DIM]
                msg[2 * g + 1, start : start + HEAD_DIM] = turned[HEAD_DIM:]
    for h in range(heads):
        cols = slice(LANES * (h // 2), LANES * (h // 2) + LANES)
        top, bottom = k[:half, cols], k[half:, cols]
        if h % 2 == 0:
            bottom = swap_halves(bottom)
        else:
            top = swap_halves(top)
        msg[h, :half] = jnp.where(low, top, bottom).astype(jnp.bfloat16)
    for j in range(heads):
        if j < near:
            outs[j][...] = msg[a ^ j]
        else:
            outs[j][...] = msg[a ^ j, :rows]
            outs[heads + j - near][...] = msg[a ^ j, rows:]


def list_kernel(inner, outer, per, cap, parts, mask, order, who, which, valid, first, steps, names, load):
    c = lax.axis_index("ctx")
    a = c // inner
    b = (c % inner) // 2 * 2 + lax.axis_index("head") % 2
    blocks = inner * outer * per
    half = per // 2
    size = outer * per // parts

    def name(dev, _):
        kb = ((lax.div(dev, inner) ^ a) * inner + (lax.rem(dev, inner) ^ b)) * per
        for i in range(per):
            names[dev * per + i] = order[kb + i // 2 + i % 2 * half]
        return 0

    lax.fori_loop(0, inner * outer, name, 0)
    for part in range(parts):
        for s in range(STREAMS):
            load[s] = 0

        def row(qi, _):
            qb = ((lax.div(qi, per) ^ a) * inner + b) * per + lax.rem(qi, per)
            own = order[qb]
            s, least = jnp.int32(0), load[0]
            for other in range(1, STREAMS):
                here = load[other]
                s = jnp.where(here < least, other, s)
                least = jnp.minimum(here, least)
            item = (part * STREAMS + s) * cap + least
            base = item * SLOTS

            def col(n, to):
                for e in range(8):
                    slot = n * 8 + e
                    which[to] = slot
                    to = to + mask[own, names[slot]]
                return to

            end = lax.fori_loop(0, blocks // 8, col, base)
            count = end - base
            keep = which[base]
            for extra in range(SLOTS):
                which[end + extra] = keep
            items = lax.div(count + (SLOTS - 1), SLOTS)

            def mark(t, left):
                who[item + t] = qi - part * size
                valid[item + t] = left
                first[item + t] = 0
                return left - SLOTS

            lax.fori_loop(0, items, mark, count)
            first[item] = 1
            load[s] = least + items
            return 0

        lax.fori_loop(part * size, (part + 1) * size, row, 0)
        most = load[0]
        for s in range(1, STREAMS):
            most = jnp.maximum(most, load[s])
        steps[part] = most
        for s in range(STREAMS):
            start = (part * STREAMS + s) * cap
            last = start + jnp.maximum(load[s] - 1, 0)
            idle = load[s] == 0
            qi = jnp.where(idle, size, who[last])
            key = jnp.where(idle, 0, which[last * SLOTS])

            def fill(t, _):
                at = start + t
                who[at] = qi
                valid[at] = 0
                first[at] = 0
                for e in range(SLOTS):
                    which[at * SLOTS + e] = key
                return 0

            lax.fori_loop(load[s], most + 2, fill, 0)


def attend_kernel(part, per, cap, n_kv, spans, who, which, valid, first, steps, *rest):
    ins, rest = rest[:n_kv], rest[n_kv:]
    q_in, rest = rest[: len(spans)], rest[len(spans) :]
    outs, rest = rest[: len(spans)], rest[len(spans) :]
    if part == 0:
        (kq, vt), rest = rest[:2], rest[2:]
    else:
        kq, vt = ins
    qt, sc, m_s, al_s, l_s, acc_s, l_all, acc_all = rest
    half = per // 2
    nq = len(spans) * per
    zero = jnp.zeros((HEAD_DIM, BLOCK), jnp.bfloat16)
    for k, start in enumerate(spans):
        for i in range(per):
            turned = q_in[k][start + i * HEAD_DIM : start + (i + 1) * HEAD_DIM, :]
            qt[0, k * per + i] = jnp.concatenate([turned, zero], axis=0)
            qt[1, k * per + i] = jnp.concatenate([zero, turned], axis=0)
    qt[:, nq] = jnp.zeros((2, LANES, BLOCK), jnp.bfloat16)
    if part == 0:
        for n, msg in enumerate(ins):
            for r in range(half):
                kq[n * half + r] = msg[r * BLOCK : (r + 1) * BLOCK, :]
            for i in range(per):
                start = half * BLOCK + (i // 2 + i % 2 * half) * HEAD_DIM
                vt[n * per + i] = msg[start : start + HEAD_DIM, :]
    m_s[...] = jnp.full(m_s.shape, NEG, jnp.float32)
    l_s[...] = jnp.zeros(l_s.shape, jnp.float32)
    acc_s[...] = jnp.zeros(acc_s.shape, jnp.float32)

    def keys(s, t):
        return [which[((part * STREAMS + s) * cap + t) * SLOTS + e] for e in range(SLOTS)]

    def score(t, buf):
        for s in range(STREAMS):
            qi = who[(part * STREAMS + s) * cap + t]
            tiles = []
            for e, slot in enumerate(keys(s, t)):
                tile = jnp.dot(
                    kq[slot >> 1], qt[slot & 1, qi], preferred_element_type=jnp.float32
                )
                sc[buf, s, e] = tile
                tiles.append(tile.reshape(BLOCK // 8, 8, BLOCK))
            top = jnp.max(functools.reduce(jnp.maximum, tiles), axis=0)
            top = jnp.max(top, axis=0, keepdims=True)
            m_old = jnp.where(first[(part * STREAMS + s) * cap + t] == 1, NEG, m_s[1 - buf, s])
            m_new = jnp.maximum(m_old, top)
            al_s[buf, s] = jnp.exp(m_old - m_new)
            m_s[buf, s] = m_new

    def weigh(t, buf):
        for s in range(STREAMS):
            qi = who[(part * STREAMS + s) * cap + t]
            n_valid = valid[(part * STREAMS + s) * cap + t]
            m, alpha = m_s[buf, s], al_s[buf, s]
            acc = acc_s[s] * alpha
            total = l_s[s] * alpha
            ids = keys(s, t)
            for e in range(0, SLOTS, 2):
                probs = []
                for f in (e, e + 1):
                    shut = m + jnp.where(f < n_valid, 0.0, -NEG)
                    p = jnp.exp(sc[buf, s, f] - shut)
                    total = total + jnp.sum(p.reshape(BLOCK // 8, 8, BLOCK), axis=0)
                    probs.append(p.astype(jnp.bfloat16))
                acc = acc + jnp.dot(
                    jnp.concatenate([vt[ids[e]], vt[ids[e + 1]]], axis=1),
                    jnp.concatenate(probs, axis=0),
                    preferred_element_type=jnp.float32,
                )
            acc_s[s] = acc
            l_s[s] = total
            acc_all[qi] = acc
            l_all[qi] = total

    score(0, 0)

    def step(u, _):
        t = 2 * u
        score(t + 1, 1)
        weigh(t, 0)
        score(t + 2, 0)
        weigh(t + 1, 1)
        return 0

    lax.fori_loop(0, lax.div(steps[part] + 1, 2), step, 0)
    for k in range(len(spans)):
        for r in range(half):
            done = []
            for i in (k * per + r, k * per + r + half):
                done.append(acc_all[i] * (1.0 / jnp.sum(l_all[i], axis=0, keepdims=True)))
            outs[k][r * BLOCK : (r + 1) * BLOCK, :] = jnp.transpose(
                jnp.concatenate(done, axis=0)
            ).astype(jnp.bfloat16)


def out_kernel(inner, heads, groups, *refs):
    pieces = [refs[g * heads : (g + 1) * heads] for g in range(groups)]
    ws = refs[groups * heads : groups * heads + groups]
    out = refs[-1]
    a = lax.axis_index("ctx") // inner
    half = pieces[0][0].shape[0]
    low = low_half((half, LANES))
    tops, bottoms, rows = [], [], []
    for g in range(groups):
        for k in range(0, heads, 2):
            p0 = pieces[g][k][...].astype(jnp.float32)
            p1 = pieces[g][k + 1][...].astype(jnp.float32)
            tops.append(jnp.where(low, p0, swap_halves(p1)).astype(jnp.bfloat16))
            bottoms.append(jnp.where(low, swap_halves(p0), p1).astype(jnp.bfloat16))
            for e in (0, 1):
                start = pl.multiple_of(HEAD_DIM * (a ^ (k + e)), HEAD_DIM)
                rows.append(ws[g][pl.ds(start, HEAD_DIM), :])
    w = jnp.concatenate(rows, axis=0)
    for n, parts in enumerate((tops, bottoms)):
        x = jnp.concatenate(parts, axis=1)
        out[n * half : (n + 1) * half, :] = jnp.dot(
            x, w, preferred_element_type=jnp.float32
        ).astype(out.dtype)


def solution(mesh):
    ctx, groups = mesh.shape["ctx"], mesh.shape["head"]

    def body(tokens, w_query, w_key, w_value, w_out, block_mask, block_order):
        rows = tokens.shape[0]
        heads = w_query.shape[1] // HEAD_DIM
        inner = ctx // heads
        per = rows // BLOCK
        nb = block_mask.shape[0]
        nq = heads * per
        cols = w_out.shape[1] // groups
        bf = jnp.bfloat16
        params = pltpu.CompilerParams(vmem_limit_bytes=GRANT)
        both = ("ctx", "head")
        places = [(c // inner, c % inner, h) for c in range(ctx) for h in range(groups)]

        def index(a, b, h):
            return (a * inner + b) * groups + h

        def turn(x, j):
            pairs = [
                (index(a, b, h), index(a ^ j, (b & ~1) | (h & 1), (h & ~1) | (b & 1)))
                for a, b, h in places
            ]
            return lax.ppermute(x, both, pairs)

        def spread(x, e):
            pairs = [
                (index(a, b, h), index(a, b ^ (e & ~1), h ^ (e & 1))) for a, b, h in places
            ]
            return lax.ppermute(x, both, pairs) if e else x

        def head_swap(x, j):
            return lax.ppermute(x, "head", [(h, h ^ j) for h in range(groups)]) if j else x

        half, size = rows // 2, rows + rows // 2
        near = heads // 2
        sizes = [size] * near + [rows] * (heads - near) + [half] * (heads - near)
        msgs = pl.pallas_call(
            functools.partial(proj_kernel, inner, heads, near),
            out_shape=[jax.ShapeDtypeStruct((n, LANES), bf) for n in sizes],
            in_specs=[HBM] * 4,
            out_specs=[VMEM] * len(sizes),
            scratch_shapes=[pltpu.VMEM(x.shape, bf) for x in (tokens, w_value, w_key, w_query)]
            + [
                pltpu.VMEM((heads, size, LANES), bf),
                pltpu.SemaphoreType.DMA((4,)),
            ],
            compiler_params=pltpu.CompilerParams(vmem_limit_bytes=WHOLE),
            name="proj",
        )(tokens, w_key, w_value, w_query)
        got, late = [None] * heads, [None] * heads
        for j in reversed(range(heads)):
            got[j] = turn(msgs[j], j)
        for j in range(near, heads):
            late[j] = turn(msgs[heads + j - near], j)
        parts = heads // near
        longest = -(-nb // SLOTS)
        cap = -(-nq // parts * longest // STREAMS) + longest + 3
        tables = pl.pallas_call(
            functools.partial(list_kernel, inner, heads, per, cap, parts),
            out_shape=[
                jax.ShapeDtypeStruct((parts * STREAMS * cap,), jnp.int32),
                jax.ShapeDtypeStruct((parts * STREAMS * cap * SLOTS,), jnp.int32),
                jax.ShapeDtypeStruct((parts * STREAMS * cap,), jnp.int32),
                jax.ShapeDtypeStruct((parts * STREAMS * cap,), jnp.int32),
                jax.ShapeDtypeStruct((parts,), jnp.int32),
            ],
            in_specs=[SMEM] * 2,
            out_specs=[SMEM] * 5,
            scratch_shapes=[pltpu.SMEM((nb,), jnp.int32), pltpu.SMEM((STREAMS,), jnp.int32)],
            name="block_lists",
        )(block_mask, block_order)
        h = lax.axis_index("head")
        w_out, msgs = lax.optimization_barrier((w_out, msgs))
        w_cols = []
        for j in range(groups):
            part = lax.dynamic_slice_in_dim(w_out, (h ^ j) * cols, cols, axis=1)
            w_cols.append(head_swap(part, j))
        got[0], tables, w_cols = lax.optimization_barrier((got[0], tables, w_cols))
        kv = [spread(got[j], e) for j in range(heads) for e in range(inner)]
        o = []
        for part in range(parts):
            if part == 0:
                queries, spans = got[:near], (rows,) * near
                extra = [
                    jax.ShapeDtypeStruct((nb // 2, BLOCK, LANES), bf),
                    jax.ShapeDtypeStruct((nb, HEAD_DIM, BLOCK), bf),
                ]
            else:
                queries, spans, extra = late[part * near : (part + 1) * near], (0,) * near, []
            mini = near * per + 1
            made = pl.pallas_call(
                functools.partial(attend_kernel, part, per, cap, len(kv), spans),
                out_shape=[jax.ShapeDtypeStruct((half, LANES), bf)] * near + extra,
                in_specs=[SMEM] * 5 + [VMEM] * (len(kv) + near),
                out_specs=[VMEM] * (near + len(extra)),
                scratch_shapes=[
                    pltpu.VMEM((2, mini, LANES, BLOCK), bf),
                    pltpu.VMEM((2, STREAMS, SLOTS, BLOCK, BLOCK), jnp.float32),
                    pltpu.VMEM((2, STREAMS, 1, BLOCK), jnp.float32),
                    pltpu.VMEM((2, STREAMS, 1, BLOCK), jnp.float32),
                    pltpu.VMEM((STREAMS, 8, BLOCK), jnp.float32),
                    pltpu.VMEM((STREAMS, HEAD_DIM, BLOCK), jnp.float32),
                    pltpu.VMEM((mini, 8, BLOCK), jnp.float32),
                    pltpu.VMEM((mini, HEAD_DIM, BLOCK), jnp.float32),
                ],
                compiler_params=params,
            )(*tables, *kv, *queries)
            o += made[:near]
            if part == 0:
                kv = made[near:]
        mine = [None] * heads
        for j in reversed(range(heads)):
            mine[j] = turn(o[j], j)
        parts = [mine]
        for g in range(1, groups):
            part = []
            for j in range(heads):
                if g % 2:
                    part.append(head_swap(parts[g - 1][j], 1))
                else:
                    part.append(head_swap(mine[j], g))
            parts.append(part)
        return pl.pallas_call(
            functools.partial(out_kernel, inner, heads, groups),
            out_shape=jax.ShapeDtypeStruct((rows, cols), bf),
            in_specs=[VMEM] * (groups * heads + groups),
            out_specs=VMEM,
            compiler_params=params,
            name="out_proj",
        )(*[x for part in parts for x in part], *w_cols)

    placed = (
        P("ctx", None),
        P(None, "head"),
        P(None, "head"),
        P(None, "head"),
        P("head", None),
        P(),
        P(),
    )
    return jax.shard_map(
        body, mesh=mesh, in_specs=placed, out_specs=P("ctx", "head"), check_vma=False
    )
```

profile of v0, /device:TPU:0, one launch (start us, length us, event | category | flops | bytes accessed | tf_op | source)
XLA Modules:
  0.0 61.9 jit_solution(17404121212652994600)
XLA Ops:
  0.0 3.6 %proj.1 = (bf16[768,128]{1,0:T(8,128)(2,1)}, bf16[768,128]{1,0:T(8,128)(2,1)}, bf16[512,128]{1,0:T(8,128)(2,1)}, bf16[512,128]{1,0:T(8,128)(2,1)}, bf16[256,128]{1,0:T(8,128)(2,1)}, /*index=5*/bf16[256,128]{1,0:T(8,128)(2,1)}) custom-call(bf16[512,1024]{1,0:T(8,128)(2,1)} %tok_in.1, bf16[1024,256]{1,0:T(8,128)(2,1)} %wk_in.1, bf16[1024,256]{1,0:T(8,128)(2,1)} %wv_in.1, ...), custom_call_target="tpu_custom_call" | custom-call | tf_op jit(solution)/shard_map/proj/pallas_call | solution.py:315
  3.7 1.6 %collective-permute-start = (bf16[768,128]{1,0:T(8,128)(2,1)}, bf16[768,128]{1,0:T(8,128)(2,1)S(1)}, u32[]{:S(2)}, u32[]{:S(2)}) collective-permute-start(bf16[768,128]{1,0:T(8,128)(2,1)} %get-tuple-element.33), channel_id=1, source_target_pairs={{0,0},{1,4},{2,2},{3,6},{4,1},{5,5},{6,3},{7,7},{8,8},{9,12},{10,1... | collective-permute-start | bytes 589832 | tf_op jit(solution)/shard_map/ppermute | solution.py:301
  5.3 0.1 constant_dynamic-slice_fusion
  5.4 4.6 %collective-permute-start.3 = (bf16[256,256]{1,0:T(8,128)(2,1)S(1)}, bf16[256,256]{1,0:T(8,128)(2,1)S(1)}, u32[]{:S(2)}, u32[]{:S(2)}) collective-permute-start(bf16[256,256]{1,0:T(8,128)(2,1)S(1)} %get-tuple-element.61), channel_id=1, source_target_pairs={{0,3},{1,2},{2,1},{3,0},{4,7},{5,6},{6,5},{7,4},{8,11},{9,10},{10,... | collective-permute-start | bytes 393224 | tf_op jit(solution)/shard_map/ppermute | solution.py:310
  10.0 0.5 collective-permute-start.2
  10.5 1.6 %collective-permute-start.5 = (bf16[768,128]{1,0:T(8,128)(2,1)S(1)}, bf16[768,128]{1,0:T(8,128)(2,1)S(1)}, u32[]{:S(2)}, u32[]{:S(2)}) collective-permute-start(bf16[768,128]{1,0:T(8,128)(2,1)S(1)} %copy-done.6), channel_id=1, source_target_pairs={{0,8},{1,12},{2,10},{3,14},{4,9},{5,13},{6,11},{7,15},{8,0},{9,4},... | collective-permute-start | bytes 589832 | tf_op jit(solution)/shard_map/ppermute | solution.py:301
  12.1 0.0 collective-permute-start.1
  12.1 1.4 %collective-permute-done.3.refs_19_ = bf16[256,256]{1,0:T(8,128)(2,1)S(1)} collective-permute-done((bf16[256,256]{1,0:T(8,128)(2,1)S(1)}, bf16[256,256]{1,0:T(8,128)(2,1)S(1)}, u32[]{:S(2)}, u32[]{:S(2)}) %collective-permute-start.3) | collective-permute-done | bytes 131104 | tf_op jit(solution)/shard_map/ppermute | solution.py:310
  13.5 2.6 %collective-permute-start.7 = (bf16[512,128]{1,0:T(8,128)(2,1)S(1)}, bf16[512,128]{1,0:T(8,128)(2,1)S(1)}, u32[]{:S(2)}, u32[]{:S(2)}) collective-permute-start(bf16[512,128]{1,0:T(8,128)(2,1)S(1)} %copy-done.8), channel_id=1, source_target_pairs={{0,16},{1,20},{2,18},{3,22},{4,17},{5,21},{6,19},{7,23},{8,24},{9,... | collective-permute-start | bytes 393224 | tf_op jit(solution)/shard_map/ppermute | solution.py:301
  16.1 0.8 %collective-permute-done.2.refs_18_ = bf16[256,256]{1,0:T(8,128)(2,1)S(1)} collective-permute-done((bf16[256,256]{1,0:T(8,128)(2,1)S(1)}, bf16[256,256]{1,0:T(8,128)(2,1)S(1)}, u32[]{:S(2)}, u32[]{:S(2)}) %collective-permute-start.2) | collective-permute-done | bytes 131104 | tf_op jit(solution)/shard_map/ppermute | solution.py:310
  16.9 3.6 %collective-permute-start.9 = (bf16[512,128]{1,0:T(8,128)(2,1)S(1)}, bf16[512,128]{1,0:T(8,128)(2,1)S(1)}, u32[]{:S(2)}, u32[]{:S(2)}) collective-permute-start(bf16[512,128]{1,0:T(8,128)(2,1)S(1)} %copy-done.7), channel_id=1, source_target_pairs={{0,24},{1,28},{2,26},{3,30},{4,25},{5,29},{6,27},{7,31},{8,16},{9,... | collective-permute-start | bytes 393224 | tf_op jit(solution)/shard_map/ppermute | solution.py:301
  20.5 4.5 %block_lists.1 = (s32[216]{0:T(256)}, s32[864]{0:T(1024)}, s32[216]{0:T(256)}, s32[216]{0:T(256)}, s32[2]{0:T(128)}) custom-call(s32[32,32]{1,0:T(8,128)} %mask.1, s32[32]{0:T(128)} %order.1), custom_call_target="tpu_custom_call" | custom-call | tf_op jit(solution)/shard_map/block_lists/pallas_call | solution.py:336
  25.0 0.0 collective-permute-done.1.refs_17_
  25.0 0.0 collective-permute-done.rest_0_.rest_8_
  25.1 0.0 collective-permute-done.5.rest_2_.rest_9_
  25.1 0.1 collective-permute-start.6
  25.2 0.5 collective-permute-start.4
  25.7 0.3 collective-permute-done.7.rest_4_
  26.0 1.3 %collective-permute-start.8 = (bf16[512,128]{1,0:T(8,128)(2,1)S(1)}, bf16[512,128]{1,0:T(8,128)(2,1)S(1)}, u32[]{:S(2)}, u32[]{:S(2)}) collective-permute-start(bf16[512,128]{1,0:T(8,128)(2,1)S(1)} %collective-permute-done.7.rest_4_), channel_id=1, source_target_pairs={{0,1},{1,0},{2,3},{3,2},{4,5},{5,4},{6,7},{7,6},{8,9},{9,8},{10,11... | collective-permute-start | bytes 393224 | tf_op jit(solution)/shard_map/ppermute | solution.py:307
  27.3 0.0 collective-permute-done.9.rest_6_
  27.3 0.0 collective-permute-start.10
  27.3 4.4 %collective-permute-start.13 = (bf16[256,128]{1,0:T(8,128)(2,1)S(1)}, bf16[256,128]{1,0:T(8,128)(2,1)S(1)}, u32[]{:S(2)}, u32[]{:S(2)}) collective-permute-start(bf16[256,128]{1,0:T(8,128)(2,1)S(1)} %copy-done.10), channel_id=1, source_target_pairs={{0,16},{1,20},{2,18},{3,22},{4,17},{5,21},{6,19},{7,23},{8,24},{9,... | collective-permute-start | bytes 196616 | tf_op jit(solution)/shard_map/ppermute | solution.py:301
  31.7 0.0 collective-permute-done.8.rest_5_
  31.7 0.6 collective-permute-start.14
  32.3 0.0 collective-permute-done.10.rest_7_
  32.3 0.0 collective-permute-done.6.rest_3_
  32.3 0.0 collective-permute-done.4.rest_1_
  32.3 3.0 %shard_map.73 = (bf16[256,128]{1,0:T(8,128)(2,1)S(1)}, bf16[256,128]{1,0:T(8,128)(2,1)S(1)}, bf16[16,128,128]{2,1,0:T(8,128)(2,1)S(1)}, bf16[32,64,128]{2,1,0:T(8,128)(2,1)S(1)}) custom-call(s32[216]{0:T(256)S(1)} %copy-done.1, s32[864]{0:T(1024)S(1)} %copy-done, s32[216]{0:T(256)S(1)} %copy-done.2, s32[216]{0:T(256)S(1)} %copy-done.3, s32[2]{0:T(128)S(1)} %copy-done.4, ...), custom_call_target="tpu_custom_call" | custom-call | tf_op jit(solution)/shard_map/pallas_call | solution.py:369
  35.4 0.7 %collective-permute-start.11 = (bf16[256,128]{1,0:T(8,128)(2,1)S(1)}, bf16[256,128]{1,0:T(8,128)(2,1)S(1)}, u32[]{:S(2)}, u32[]{:S(2)}) collective-permute-start(bf16[256,128]{1,0:T(8,128)(2,1)S(1)} %get-tuple-element.51), channel_id=1, source_target_pairs={{0,0},{1,4},{2,2},{3,6},{4,1},{5,5},{6,3},{7,7},{8,8},{9,12},{10,1... | collective-permute-start | bytes 196616 | tf_op jit(solution)/shard_map/ppermute | solution.py:301
  36.1 0.2 collective-permute-start.12
  36.2 0.0 collective-permute-done.13.rest_2_
  36.2 1.9 %collective-permute-done.14.rest_3_ = bf16[256,128]{1,0:T(8,128)(2,1)S(1)} collective-permute-done((bf16[256,128]{1,0:T(8,128)(2,1)S(1)}, bf16[256,128]{1,0:T(8,128)(2,1)S(1)}, u32[]{:S(2)}, u32[]{:S(2)}) %collective-permute-start.14) | collective-permute-done | bytes 65568 | tf_op jit(solution)/shard_map/ppermute | solution.py:301
  38.2 3.9 %shard_map.74 = (bf16[256,128]{1,0:T(8,128)(2,1)S(1)}, bf16[256,128]{1,0:T(8,128)(2,1)S(1)}) custom-call(s32[216]{0:T(256)S(1)} %copy-done.1, s32[864]{0:T(1024)S(1)} %copy-done, s32[216]{0:T(256)S(1)} %copy-done.2, s32[216]{0:T(256)S(1)} %copy-done.3, s32[2]{0:T(128)S(1)} %copy-done.4, bf16[16,128,128]{2,1,0:T(8,128)(2,1)S(1)} %get-tuple-element.53.rest_0_, ...), custom_call_target="tpu_custom_call" | custom-call | tf_op jit(solution)/shard_map/pallas_call | solution.py:369
  42.0 1.9 %collective-permute-start.15 = (bf16[256,128]{1,0:T(8,128)(2,1)S(1)}, bf16[256,128]{1,0:T(8,128)(2,1)S(1)}, u32[]{:S(2)}, u32[]{:S(2)}) collective-permute-start(bf16[256,128]{1,0:T(8,128)(2,1)S(1)} %get-tuple-element.55), channel_id=1, source_target_pairs={{0,16},{1,20},{2,18},{3,22},{4,17},{5,21},{6,19},{7,23},{8,24},{9,... | collective-permute-start | bytes 196616 | tf_op jit(solution)/shard_map/ppermute | solution.py:301
  43.9 1.6 %collective-permute-start.16 = (bf16[256,128]{1,0:T(8,128)(2,1)S(1)}, bf16[256,128]{1,0:T(8,128)(2,1)S(1)}, u32[]{:S(2)}, u32[]{:S(2)}) collective-permute-start(bf16[256,128]{1,0:T(8,128)(2,1)S(1)} %get-tuple-element.56), channel_id=1, source_target_pairs={{0,24},{1,28},{2,26},{3,30},{4,25},{5,29},{6,27},{7,31},{8,16},{9,... | collective-permute-start | bytes 196616 | tf_op jit(solution)/shard_map/ppermute | solution.py:301
  45.6 0.0 collective-permute-done.11.refs_0_
  45.6 1.0 %collective-permute-start.21 = (bf16[256,128]{1,0:T(8,128)(2,1)S(1)}, bf16[256,128]{1,0:T(8,128)(2,1)S(1)}, u32[]{:S(2)}, u32[]{:S(2)}) collective-permute-start(bf16[256,128]{1,0:T(8,128)(2,1)S(1)} %collective-permute-done.11.refs_0_), channel_id=1, source_target_pairs={{0,2},{1,3},{2,0},{3,1},{4,6},{5,7},{6,4},{7,5},{8,10},{9,11},{10,... | collective-permute-start | bytes 196616 | tf_op jit(solution)/shard_map/ppermute | solution.py:310
  46.5 2.7 %collective-permute-start.17 = (bf16[256,128]{1,0:T(8,128)(2,1)S(1)}, bf16[256,128]{1,0:T(8,128)(2,1)S(1)}, u32[]{:S(2)}, u32[]{:S(2)}) collective-permute-start(bf16[256,128]{1,0:T(8,128)(2,1)S(1)} %collective-permute-done.11.refs_0_), channel_id=1, source_target_pairs={{0,1},{1,0},{2,3},{3,2},{4,5},{5,4},{6,7},{7,6},{8,9},{9,8},{10,11... | collective-permute-start | bytes 196616 | tf_op jit(solution)/shard_map/ppermute | solution.py:310
  49.2 0.0 collective-permute-done.12.refs_1_
  49.2 1.1 %collective-permute-start.22 = (bf16[256,128]{1,0:T(8,128)(2,1)S(1)}, bf16[256,128]{1,0:T(8,128)(2,1)S(1)}, u32[]{:S(2)}, u32[]{:S(2)}) collective-permute-start(bf16[256,128]{1,0:T(8,128)(2,1)S(1)} %collective-permute-done.12.refs_1_), channel_id=1, source_target_pairs={{0,2},{1,3},{2,0},{3,1},{4,6},{5,7},{6,4},{7,5},{8,10},{9,11},{10,... | collective-permute-start | bytes 196616 | tf_op jit(solution)/shard_map/ppermute | solution.py:310
  50.3 0.0 collective-permute-done.15.refs_2_
  50.3 0.5 collective-permute-start.18
  50.8 0.0 collective-permute-done.16.refs_3_
  50.8 0.9 %collective-permute-start.23 = (bf16[256,128]{1,0:T(8,128)(2,1)S(1)}, bf16[256,128]{1,0:T(8,128)(2,1)S(1)}, u32[]{:S(2)}, u32[]{:S(2)}) collective-permute-start(bf16[256,128]{1,0:T(8,128)(2,1)S(1)} %collective-permute-done.15.refs_2_), channel_id=1, source_target_pairs={{0,2},{1,3},{2,0},{3,1},{4,6},{5,7},{6,4},{7,5},{8,10},{9,11},{10,... | collective-permute-start | bytes 196616 | tf_op jit(solution)/shard_map/ppermute | solution.py:310
  51.7 0.0 collective-permute-done.21.refs_8_
  51.7 3.4 %collective-permute-start.19 = (bf16[256,128]{1,0:T(8,128)(2,1)S(1)}, bf16[256,128]{1,0:T(8,128)(2,1)S(1)}, u32[]{:S(2)}, u32[]{:S(2)}) collective-permute-start(bf16[256,128]{1,0:T(8,128)(2,1)S(1)} %collective-permute-done.15.refs_2_), channel_id=1, source_target_pairs={{0,1},{1,0},{2,3},{3,2},{4,5},{5,4},{6,7},{7,6},{8,9},{9,8},{10,11... | collective-permute-start | bytes 196616 | tf_op jit(solution)/shard_map/ppermute | solution.py:310
  55.1 0.0 collective-permute-done.17.refs_4_
  55.1 1.0 %collective-permute-start.24 = (bf16[256,128]{1,0:T(8,128)(2,1)S(1)}, bf16[256,128]{1,0:T(8,128)(2,1)S(1)}, u32[]{:S(2)}, u32[]{:S(2)}) collective-permute-start(bf16[256,128]{1,0:T(8,128)(2,1)S(1)} %collective-permute-done.16.refs_3_), channel_id=1, source_target_pairs={{0,2},{1,3},{2,0},{3,1},{4,6},{5,7},{6,4},{7,5},{8,10},{9,11},{10,... | collective-permute-start | bytes 196616 | tf_op jit(solution)/shard_map/ppermute | solution.py:310
  56.1 0.0 collective-permute-done.22.refs_9_
  56.1 0.0 collective-permute-start.20
  56.1 0.0 collective-permute-done.18.refs_5_
  56.1 0.5 collective-permute-start.25
  56.6 0.0 collective-permute-done.23.refs_10_
  56.6 0.8 %collective-permute-start.26 = (bf16[256,128]{1,0:T(8,128)(2,1)S(1)}, bf16[256,128]{1,0:T(8,128)(2,1)S(1)}, u32[]{:S(2)}, u32[]{:S(2)}) collective-permute-start(bf16[256,128]{1,0:T(8,128)(2,1)S(1)} %collective-permute-done.22.refs_9_), channel_id=1, source_target_pairs={{0,1},{1,0},{2,3},{3,2},{4,5},{5,4},{6,7},{7,6},{8,9},{9,8},{10,11... | collective-permute-start | bytes 196616 | tf_op jit(solution)/shard_map/ppermute | solution.py:310
  57.5 0.0 collective-permute-done.19.refs_6_
  57.5 0.0 collective-permute-start.27
  57.5 1.9 %collective-permute-done.24.refs_11_ = bf16[256,128]{1,0:T(8,128)(2,1)S(1)} collective-permute-done((bf16[256,128]{1,0:T(8,128)(2,1)S(1)}, bf16[256,128]{1,0:T(8,128)(2,1)S(1)}, u32[]{:S(2)}, u32[]{:S(2)}) %collective-permute-start.24) | collective-permute-done | bytes 65568 | tf_op jit(solution)/shard_map/ppermute | solution.py:310
  59.4 0.0 collective-permute-start.28
  59.4 0.0 collective-permute-done.20.refs_7_
  59.4 0.0 collective-permute-done.25.refs_12_
  59.4 0.0 collective-permute-done.26.refs_13_
  59.4 0.0 collective-permute-done.27.refs_14_
  59.4 1.2 %collective-permute-done.28.refs_15_ = bf16[256,128]{1,0:T(8,128)(2,1)S(1)} collective-permute-done((bf16[256,128]{1,0:T(8,128)(2,1)S(1)}, bf16[256,128]{1,0:T(8,128)(2,1)S(1)}, u32[]{:S(2)}, u32[]{:S(2)}) %collective-permute-start.28) | collective-permute-done | bytes 65568 | tf_op jit(solution)/shard_map/ppermute | solution.py:310
  60.6 1.3 %out_proj.1 = bf16[512,256]{1,0:T(8,128)(2,1)} custom-call(bf16[256,128]{1,0:T(8,128)(2,1)S(1)} %collective-permute-done.11.refs_0_, bf16[256,128]{1,0:T(8,128)(2,1)S(1)} %collective-permute-done.12.refs_1_, bf16[256,128]{1,0:T(8,128)(2,1)S(1)} %collective-permute-done.15.refs_2_, bf16[256,128]{1,0:T(8,128)(2,1)S(1)} %collective-permute-done.16.refs_3_, ...), custom_call_target="tpu_custom_call" | custom-call | tf_op jit(solution)/shard_map/out_proj/pallas_call | solution.py:401
  (22 shorter events, 0.0 us)
Async XLA Ops:
  0.0 5.2 %copy-start.5 = (bf16[256,1024]{1,0:T(8,128)(2,1)S(1)}, bf16[256,1024]{1,0:T(8,128)(2,1)}, u32[]{:S(2)}) copy-start(bf16[256,1024]{1,0:T(8,128)(2,1)} %param.11) | copy-start | bytes 1572868
  3.7 21.4 %collective-permute-start = (bf16[768,128]{1,0:T(8,128)(2,1)}, bf16[768,128]{1,0:T(8,128)(2,1)S(1)}, u32[]{:S(2)}, u32[]{:S(2)}) collective-permute-start(bf16[768,128]{1,0:T(8,128)(2,1)} %get-tuple-element.33), channel_id=1, source_target_pairs={{0,0},{1,4},{2,2},{3,6},{4,1},{5,5},{6,3},{7,7},{8,8},{9,12},{10,1... | collective-permute-start | bytes 589832 | tf_op jit(solution)/shard_map/ppermute | solution.py:301
  5.2 5.3 %copy-start.6 = (bf16[768,128]{1,0:T(8,128)(2,1)S(1)}, bf16[768,128]{1,0:T(8,128)(2,1)}, u32[]{:S(2)}) copy-start(bf16[768,128]{1,0:T(8,128)(2,1)} %get-tuple-element.39) | copy-start | bytes 589828
  5.2 8.3 %copy-start.8 = (bf16[512,128]{1,0:T(8,128)(2,1)S(1)}, bf16[512,128]{1,0:T(8,128)(2,1)}, u32[]{:S(2)}) copy-start(bf16[512,128]{1,0:T(8,128)(2,1)} %get-tuple-element.40) | copy-start | bytes 393220
  5.3 11.6 %copy-start.7 = (bf16[512,128]{1,0:T(8,128)(2,1)S(1)}, bf16[512,128]{1,0:T(8,128)(2,1)}, u32[]{:S(2)}) copy-start(bf16[512,128]{1,0:T(8,128)(2,1)} %get-tuple-element.41) | copy-start | bytes 393220
  5.3 22.0 %copy-start.10 = (bf16[256,128]{1,0:T(8,128)(2,1)S(1)}, bf16[256,128]{1,0:T(8,128)(2,1)}, u32[]{:S(2)}) copy-start(bf16[256,128]{1,0:T(8,128)(2,1)} %get-tuple-element.42) | copy-start | bytes 196612
  5.3 26.5 %copy-start.9 = (bf16[256,128]{1,0:T(8,128)(2,1)S(1)}, bf16[256,128]{1,0:T(8,128)(2,1)}, u32[]{:S(2)}) copy-start(bf16[256,128]{1,0:T(8,128)(2,1)} %get-tuple-element.43) | copy-start | bytes 196612
  5.4 8.2 %collective-permute-start.3 = (bf16[256,256]{1,0:T(8,128)(2,1)S(1)}, bf16[256,256]{1,0:T(8,128)(2,1)S(1)}, u32[]{:S(2)}, u32[]{:S(2)}) collective-permute-start(bf16[256,256]{1,0:T(8,128)(2,1)S(1)} %get-tuple-element.61), channel_id=1, source_target_pairs={{0,3},{1,2},{2,1},{3,0},{4,7},{5,6},{6,5},{7,4},{8,11},{9,10},{10,... | collective-permute-start | bytes 393224 | tf_op jit(solution)/shard_map/ppermute | solution.py:310
  10.0 6.9 %collective-permute-start.2 = (bf16[256,256]{1,0:T(8,128)(2,1)S(1)}, bf16[256,256]{1,0:T(8,128)(2,1)S(1)}, u32[]{:S(2)}, u32[]{:S(2)}) collective-permute-start(bf16[256,256]{1,0:T(8,128)(2,1)S(1)} %get-tuple-element.62), channel_id=1, source_target_pairs={{0,2},{1,3},{2,0},{3,1},{4,6},{5,7},{6,4},{7,5},{8,10},{9,11},{10,... | collective-permute-start | bytes 393224 | tf_op jit(solution)/shard_map/ppermute | solution.py:310
  10.5 14.6 %collective-permute-start.5 = (bf16[768,128]{1,0:T(8,128)(2,1)S(1)}, bf16[768,128]{1,0:T(8,128)(2,1)S(1)}, u32[]{:S(2)}, u32[]{:S(2)}) collective-permute-start(bf16[768,128]{1,0:T(8,128)(2,1)S(1)} %copy-done.6), channel_id=1, source_target_pairs={{0,8},{1,12},{2,10},{3,14},{4,9},{5,13},{6,11},{7,15},{8,0},{9,4},... | collective-permute-start | bytes 589832 | tf_op jit(solution)/shard_map/ppermute | solution.py:301
  12.1 12.9 %collective-permute-start.1 = (bf16[256,256]{1,0:T(8,128)(2,1)S(1)}, bf16[256,256]{1,0:T(8,128)(2,1)S(1)}, u32[]{:S(2)}, u32[]{:S(2)}) collective-permute-start(bf16[256,256]{1,0:T(8,128)(2,1)S(1)} %get-tuple-element.63), channel_id=1, source_target_pairs={{0,1},{1,0},{2,3},{3,2},{4,5},{5,4},{6,7},{7,6},{8,9},{9,8},{10,11... | collective-permute-start | bytes 393224 | tf_op jit(solution)/shard_map/ppermute | solution.py:310
  13.5 12.4 %collective-permute-start.7 = (bf16[512,128]{1,0:T(8,128)(2,1)S(1)}, bf16[512,128]{1,0:T(8,128)(2,1)S(1)}, u32[]{:S(2)}, u32[]{:S(2)}) collective-permute-start(bf16[512,128]{1,0:T(8,128)(2,1)S(1)} %copy-done.8), channel_id=1, source_target_pairs={{0,16},{1,20},{2,18},{3,22},{4,17},{5,21},{6,19},{7,23},{8,24},{9,... | collective-permute-start | bytes 393224 | tf_op jit(solution)/shard_map/ppermute | solution.py:301
  16.9 10.4 %collective-permute-start.9 = (bf16[512,128]{1,0:T(8,128)(2,1)S(1)}, bf16[512,128]{1,0:T(8,128)(2,1)S(1)}, u32[]{:S(2)}, u32[]{:S(2)}) collective-permute-start(bf16[512,128]{1,0:T(8,128)(2,1)S(1)} %copy-done.7), channel_id=1, source_target_pairs={{0,24},{1,28},{2,26},{3,30},{4,25},{5,29},{6,27},{7,31},{8,16},{9,... | collective-permute-start | bytes 393224 | tf_op jit(solution)/shard_map/ppermute | solution.py:301
  25.1 7.2 %copy-start = (s32[864]{0:T(1024)S(1)}, s32[864]{0:T(1024)}, u32[]{:S(2)}) copy-start(s32[864]{0:T(1024)} %get-tuple-element.46.which) | copy-start | bytes 10372
  25.1 7.2 %copy-start.2 = (s32[216]{0:T(256)S(1)}, s32[216]{0:T(256)}, u32[]{:S(2)}) copy-start(s32[216]{0:T(256)} %get-tuple-element.47.valid) | copy-start | bytes 2596
  25.1 7.2 %copy-start.3 = (s32[216]{0:T(256)S(1)}, s32[216]{0:T(256)}, u32[]{:S(2)}) copy-start(s32[216]{0:T(256)} %get-tuple-element.48.first) | copy-start | bytes 2596
  25.1 7.2 %copy-start.1 = (s32[216]{0:T(256)S(1)}, s32[216]{0:T(256)}, u32[]{:S(2)}) copy-start(s32[216]{0:T(256)} %get-tuple-element.45.who) | copy-start | bytes 2596
  25.1 7.2 %copy-start.4 = (s32[2]{0:T(128)S(1)}, s32[2]{0:T(128)}, u32[]{:S(2)}) copy-start(s32[2]{0:T(128)} %get-tuple-element.49.steps) | copy-start | bytes 28
  25.1 7.2 %collective-permute-start.6 = (bf16[768,128]{1,0:T(8,128)(2,1)S(1)}, bf16[768,128]{1,0:T(8,128)(2,1)S(1)}, u32[]{:S(2)}, u32[]{:S(2)}) collective-permute-start(bf16[768,128]{1,0:T(8,128)(2,1)S(1)} %collective-permute-done.5.rest_2_.rest_9_), channel_id=1, source_target_pairs={{0,1},{1,0},{2,3},{3,2},{4,5},{5,4},{6,7},{7,6},{8,9},{9,8},{10,11... | collective-permute-start | bytes 589832 | tf_op jit(solution)/shard_map/ppermute | solution.py:307
  25.2 7.1 %collective-permute-start.4 = (bf16[768,128]{1,0:T(8,128)(2,1)S(1)}, bf16[768,128]{1,0:T(8,128)(2,1)S(1)}, u32[]{:S(2)}, u32[]{:S(2)}) collective-permute-start(bf16[768,128]{1,0:T(8,128)(2,1)S(1)} %collective-permute-done.rest_0_.rest_8_), channel_id=1, source_target_pairs={{0,1},{1,0},{2,3},{3,2},{4,5},{5,4},{6,7},{7,6},{8,9},{9,8},{10,11... | collective-permute-start | bytes 589832 | tf_op jit(solution)/shard_map/ppermute | solution.py:307
  26.0 5.8 %collective-permute-start.8 = (bf16[512,128]{1,0:T(8,128)(2,1)S(1)}, bf16[512,128]{1,0:T(8,128)(2,1)S(1)}, u32[]{:S(2)}, u32[]{:S(2)}) collective-permute-start(bf16[512,128]{1,0:T(8,128)(2,1)S(1)} %collective-permute-done.7.rest_4_), channel_id=1, source_target_pairs={{0,1},{1,0},{2,3},{3,2},{4,5},{5,4},{6,7},{7,6},{8,9},{9,8},{10,11... | collective-permute-start | bytes 393224 | tf_op jit(solution)/shard_map/ppermute | solution.py:307
  27.3 5.0 %collective-permute-start.10 = (bf16[512,128]{1,0:T(8,128)(2,1)S(1)}, bf16[512,128]{1,0:T(8,128)(2,1)S(1)}, u32[]{:S(2)}, u32[]{:S(2)}) collective-permute-start(bf16[512,128]{1,0:T(8,128)(2,1)S(1)} %collective-permute-done.9.rest_6_), channel_id=1, source_target_pairs={{0,1},{1,0},{2,3},{3,2},{4,5},{5,4},{6,7},{7,6},{8,9},{9,8},{10,11... | collective-permute-start | bytes 393224 | tf_op jit(solution)/shard_map/ppermute | solution.py:307
  27.3 8.9 %collective-permute-start.13 = (bf16[256,128]{1,0:T(8,128)(2,1)S(1)}, bf16[256,128]{1,0:T(8,128)(2,1)S(1)}, u32[]{:S(2)}, u32[]{:S(2)}) collective-permute-start(bf16[256,128]{1,0:T(8,128)(2,1)S(1)} %copy-done.10), channel_id=1, source_target_pairs={{0,16},{1,20},{2,18},{3,22},{4,17},{5,21},{6,19},{7,23},{8,24},{9,... | collective-permute-start | bytes 196616 | tf_op jit(solution)/shard_map/ppermute | solution.py:301
  31.7 6.4 %collective-permute-start.14 = (bf16[256,128]{1,0:T(8,128)(2,1)S(1)}, bf16[256,128]{1,0:T(8,128)(2,1)S(1)}, u32[]{:S(2)}, u32[]{:S(2)}) collective-permute-start(bf16[256,128]{1,0:T(8,128)(2,1)S(1)} %copy-done.9), channel_id=1, source_target_pairs={{0,24},{1,28},{2,26},{3,30},{4,25},{5,29},{6,27},{7,31},{8,16},{9,... | collective-permute-start | bytes 196616 | tf_op jit(solution)/shard_map/ppermute | solution.py:301
  35.4 10.2 %collective-permute-start.11 = (bf16[256,128]{1,0:T(8,128)(2,1)S(1)}, bf16[256,128]{1,0:T(8,128)(2,1)S(1)}, u32[]{:S(2)}, u32[]{:S(2)}) collective-permute-start(bf16[256,128]{1,0:T(8,128)(2,1)S(1)} %get-tuple-element.51), channel_id=1, source_target_pairs={{0,0},{1,4},{2,2},{3,6},{4,1},{5,5},{6,3},{7,7},{8,8},{9,12},{10,1... | collective-permute-start | bytes 196616 | tf_op jit(solution)/shard_map/ppermute | solution.py:301
  36.1 13.1 %collective-permute-start.12 = (bf16[256,128]{1,0:T(8,128)(2,1)S(1)}, bf16[256,128]{1,0:T(8,128)(2,1)S(1)}, u32[]{:S(2)}, u32[]{:S(2)}) collective-permute-start(bf16[256,128]{1,0:T(8,128)(2,1)S(1)} %get-tuple-element.52), channel_id=1, source_target_pairs={{0,8},{1,12},{2,10},{3,14},{4,9},{5,13},{6,11},{7,15},{8,0},{9,4},... | collective-permute-start | bytes 196616 | tf_op jit(solution)/shard_map/ppermute | solution.py:301
  42.0 8.2 %collective-permute-start.15 = (bf16[256,128]{1,0:T(8,128)(2,1)S(1)}, bf16[256,128]{1,0:T(8,128)(2,1)S(1)}, u32[]{:S(2)}, u32[]{:S(2)}) collective-permute-start(bf16[256,128]{1,0:T(8,128)(2,1)S(1)} %get-tuple-element.55), channel_id=1, source_target_pairs={{0,16},{1,20},{2,18},{3,22},{4,17},{5,21},{6,19},{7,23},{8,24},{9,... | collective-permute-start | bytes 196616 | tf_op jit(solution)/shard_map/ppermute | solution.py:301
  43.9 6.9 %collective-permute-start.16 = (bf16[256,128]{1,0:T(8,128)(2,1)S(1)}, bf16[256,128]{1,0:T(8,128)(2,1)S(1)}, u32[]{:S(2)}, u32[]{:S(2)}) collective-permute-start(bf16[256,128]{1,0:T(8,128)(2,1)S(1)} %get-tuple-element.56), channel_id=1, source_target_pairs={{0,24},{1,28},{2,26},{3,30},{4,25},{5,29},{6,27},{7,31},{8,16},{9,... | collective-permute-start | bytes 196616 | tf_op jit(solution)/shard_map/ppermute | solution.py:301
  45.6 6.2 %collective-permute-start.21 = (bf16[256,128]{1,0:T(8,128)(2,1)S(1)}, bf16[256,128]{1,0:T(8,128)(2,1)S(1)}, u32[]{:S(2)}, u32[]{:S(2)}) collective-permute-start(bf16[256,128]{1,0:T(8,128)(2,1)S(1)} %collective-permute-done.11.refs_0_), channel_id=1, source_target_pairs={{0,2},{1,3},{2,0},{3,1},{4,6},{5,7},{6,4},{7,5},{8,10},{9,11},{10,... | collective-permute-start | bytes 196616 | tf_op jit(solution)/shard_map/ppermute | solution.py:310
  46.5 8.6 %collective-permute-start.17 = (bf16[256,128]{1,0:T(8,128)(2,1)S(1)}, bf16[256,128]{1,0:T(8,128)(2,1)S(1)}, u32[]{:S(2)}, u32[]{:S(2)}) collective-permute-start(bf16[256,128]{1,0:T(8,128)(2,1)S(1)} %collective-permute-done.11.refs_0_), channel_id=1, source_target_pairs={{0,1},{1,0},{2,3},{3,2},{4,5},{5,4},{6,7},{7,6},{8,9},{9,8},{10,11... | collective-permute-start | bytes 196616 | tf_op jit(solution)/shard_map/ppermute | solution.py:310
  49.2 6.9 %collective-permute-start.22 = (bf16[256,128]{1,0:T(8,128)(2,1)S(1)}, bf16[256,128]{1,0:T(8,128)(2,1)S(1)}, u32[]{:S(2)}, u32[]{:S(2)}) collective-permute-start(bf16[256,128]{1,0:T(8,128)(2,1)S(1)} %collective-permute-done.12.refs_1_), channel_id=1, source_target_pairs={{0,2},{1,3},{2,0},{3,1},{4,6},{5,7},{6,4},{7,5},{8,10},{9,11},{10,... | collective-permute-start | bytes 196616 | tf_op jit(solution)/shard_map/ppermute | solution.py:310
  50.3 5.8 %collective-permute-start.18 = (bf16[256,128]{1,0:T(8,128)(2,1)S(1)}, bf16[256,128]{1,0:T(8,128)(2,1)S(1)}, u32[]{:S(2)}, u32[]{:S(2)}) collective-permute-start(bf16[256,128]{1,0:T(8,128)(2,1)S(1)} %collective-permute-done.12.refs_1_), channel_id=1, source_target_pairs={{0,1},{1,0},{2,3},{3,2},{4,5},{5,4},{6,7},{7,6},{8,9},{9,8},{10,11... | collective-permute-start | bytes 196616 | tf_op jit(solution)/shard_map/ppermute | solution.py:310
  50.8 5.8 %collective-permute-start.23 = (bf16[256,128]{1,0:T(8,128)(2,1)S(1)}, bf16[256,128]{1,0:T(8,128)(2,1)S(1)}, u32[]{:S(2)}, u32[]{:S(2)}) collective-permute-start(bf16[256,128]{1,0:T(8,128)(2,1)S(1)} %collective-permute-done.15.refs_2_), channel_id=1, source_target_pairs={{0,2},{1,3},{2,0},{3,1},{4,6},{5,7},{6,4},{7,5},{8,10},{9,11},{10,... | collective-permute-start | bytes 196616 | tf_op jit(solution)/shard_map/ppermute | solution.py:310
  51.7 5.7 %collective-permute-start.19 = (bf16[256,128]{1,0:T(8,128)(2,1)S(1)}, bf16[256,128]{1,0:T(8,128)(2,1)S(1)}, u32[]{:S(2)}, u32[]{:S(2)}) collective-permute-start(bf16[256,128]{1,0:T(8,128)(2,1)S(1)} %collective-permute-done.15.refs_2_), channel_id=1, source_target_pairs={{0,1},{1,0},{2,3},{3,2},{4,5},{5,4},{6,7},{7,6},{8,9},{9,8},{10,11... | collective-permute-start | bytes 196616 | tf_op jit(solution)/shard_map/ppermute | solution.py:310
  55.1 4.3 %collective-permute-start.24 = (bf16[256,128]{1,0:T(8,128)(2,1)S(1)}, bf16[256,128]{1,0:T(8,128)(2,1)S(1)}, u32[]{:S(2)}, u32[]{:S(2)}) collective-permute-start(bf16[256,128]{1,0:T(8,128)(2,1)S(1)} %collective-permute-done.16.refs_3_), channel_id=1, source_target_pairs={{0,2},{1,3},{2,0},{3,1},{4,6},{5,7},{6,4},{7,5},{8,10},{9,11},{10,... | collective-permute-start | bytes 196616 | tf_op jit(solution)/shard_map/ppermute | solution.py:310
  56.1 3.3 %collective-permute-start.20 = (bf16[256,128]{1,0:T(8,128)(2,1)S(1)}, bf16[256,128]{1,0:T(8,128)(2,1)S(1)}, u32[]{:S(2)}, u32[]{:S(2)}) collective-permute-start(bf16[256,128]{1,0:T(8,128)(2,1)S(1)} %collective-permute-done.16.refs_3_), channel_id=1, source_target_pairs={{0,1},{1,0},{2,3},{3,2},{4,5},{5,4},{6,7},{7,6},{8,9},{9,8},{10,11... | collective-permute-start | bytes 196616 | tf_op jit(solution)/shard_map/ppermute | solution.py:310
  56.1 3.3 %collective-permute-start.25 = (bf16[256,128]{1,0:T(8,128)(2,1)S(1)}, bf16[256,128]{1,0:T(8,128)(2,1)S(1)}, u32[]{:S(2)}, u32[]{:S(2)}) collective-permute-start(bf16[256,128]{1,0:T(8,128)(2,1)S(1)} %collective-permute-done.21.refs_8_), channel_id=1, source_target_pairs={{0,1},{1,0},{2,3},{3,2},{4,5},{5,4},{6,7},{7,6},{8,9},{9,8},{10,11... | collective-permute-start | bytes 196616 | tf_op jit(solution)/shard_map/ppermute | solution.py:310
  56.6 2.8 %collective-permute-start.26 = (bf16[256,128]{1,0:T(8,128)(2,1)S(1)}, bf16[256,128]{1,0:T(8,128)(2,1)S(1)}, u32[]{:S(2)}, u32[]{:S(2)}) collective-permute-start(bf16[256,128]{1,0:T(8,128)(2,1)S(1)} %collective-permute-done.22.refs_9_), channel_id=1, source_target_pairs={{0,1},{1,0},{2,3},{3,2},{4,5},{5,4},{6,7},{7,6},{8,9},{9,8},{10,11... | collective-permute-start | bytes 196616 | tf_op jit(solution)/shard_map/ppermute | solution.py:310
  57.5 1.9 %collective-permute-start.27 = (bf16[256,128]{1,0:T(8,128)(2,1)S(1)}, bf16[256,128]{1,0:T(8,128)(2,1)S(1)}, u32[]{:S(2)}, u32[]{:S(2)}) collective-permute-start(bf16[256,128]{1,0:T(8,128)(2,1)S(1)} %collective-permute-done.23.refs_10_), channel_id=1, source_target_pairs={{0,1},{1,0},{2,3},{3,2},{4,5},{5,4},{6,7},{7,6},{8,9},{9,8},{10,11... | collective-permute-start | bytes 196616 | tf_op jit(solution)/shard_map/ppermute | solution.py:310
  59.4 1.3 %collective-permute-start.28 = (bf16[256,128]{1,0:T(8,128)(2,1)S(1)}, bf16[256,128]{1,0:T(8,128)(2,1)S(1)}, u32[]{:S(2)}, u32[]{:S(2)}) collective-permute-start(bf16[256,128]{1,0:T(8,128)(2,1)S(1)} %collective-permute-done.24.refs_11_), channel_id=1, source_target_pairs={{0,1},{1,0},{2,3},{3,2},{4,5},{5,4},{6,7},{7,6},{8,9},{9,8},{10,11... | collective-permute-start | bytes 196616 | tf_op jit(solution)/shard_map/ppermute | solution.py:310
where the time goes:
time: 62.1 us; the launch traced here: 61.9 us
  starting transfers between devices  37.7 us (61%)
  Pallas kernels  16.3 us (26%)
  waiting for transfers between devices  7.52 us (12%)
    ppermute x10, starting transfers between devices, turn(): return lax.ppermute(x, both, pairs)  18.7 us
    ppermute x15, starting transfers between devices, head_swap(): lax.ppermute(x, 'head', [(h, h ^ j) for h in range(groups)])  17.1 us
    pallas_call x2, Pallas kernels, body(): pl.pallas_call(functools.partial(attend_kernel, part, per, cap, len(kv),...  6.89 us
    ppermute x15, waiting for transfers between devices, head_swap(): lax.ppermute(x, 'head', [(h, h ^ j) for h in range(groups)])  5.29 us
    pallas_call x1, Pallas kernels, body(): pl.pallas_call(functools.partial(list_kernel, inner, heads, per, cap, par...  4.54 us
    pallas_call x1, Pallas kernels, body(): pl.pallas_call(functools.partial(proj_kernel, inner, heads, near), out_sh...  3.65 us
    ppermute x10, waiting for transfers between devices, turn(): return lax.ppermute(x, both, pairs)  2.23 us
    ppermute x4, starting transfers between devices, spread(): return lax.ppermute(x, both, pairs) if e else x  1.91 us
  transfers between devices with their start and end apart: 29, of which 6 were waited for; matrix products, arithmetic and copies ran while one was open for 0% of the time, Pallas kernels for 18%

commit v1 on v0

--- a/solution.py
+++ b/solution.py
@@ -75,13 +75,14 @@
             outs[heads + j - near][...] = msg[a ^ j, rows:]
 
 
-def list_kernel(inner, outer, per, cap, parts, mask, order, who, which, valid, first, steps, names, load):
+def list_kernel(inner, outer, per, cap, parts, mask, order, who, where, which, valid, first, steps, names, ends, load):
     c = lax.axis_index("ctx")
     a = c // inner
     b = (c % inner) // 2 * 2 + lax.axis_index("head") % 2
     blocks = inner * outer * per
     half = per // 2
     size = outer * per // parts
+    span = blocks + SLOTS
 
     def name(dev, _):
         kb = ((lax.div(dev, inner) ^ a) * inner + (lax.rem(dev, inner) ^ b)) * per
@@ -90,37 +91,49 @@
         return 0
 
     lax.fori_loop(0, inner * outer, name, 0)
+
+    def piece(k, _):
+        qb = ((k ^ a) * inner + b) * per
+        own = [order[qb + i] for i in range(per)]
+
+        def col(n, to):
+            to = list(to)
+            for e in range(8):
+                slot = n * 8 + e
+                key = names[slot]
+                for i in range(per):
+                    which[to[i]] = slot
+                    to[i] = to[i] + mask[own[i], key]
+            return tuple(to)
+
+        begin = [(k * per + i) * span for i in range(per)]
+        end = lax.fori_loop(0, blocks // 8, col, tuple(begin))
+        for i in range(per):
+            keep = which[begin[i]]
+            for extra in range(SLOTS):
+                which[end[i] + extra] = keep
+            ends[k * per + i] = end[i]
+        return 0
+
+    lax.fori_loop(0, outer, piece, 0)
     for part in range(parts):
         for s in range(STREAMS):
             load[s] = 0
 
         def row(qi, _):
-            qb = ((lax.div(qi, per) ^ a) * inner + b) * per + lax.rem(qi, per)
-            own = order[qb]
             s, least = jnp.int32(0), load[0]
             for other in range(1, STREAMS):
                 here = load[other]
                 s = jnp.where(here < least, other, s)
                 least = jnp.minimum(here, least)
             item = (part * STREAMS + s) * cap + least
-            base = item * SLOTS
-
-            def col(n, to):
-                for e in range(8):
-                    slot = n * 8 + e
-                    which[to] = slot
-                    to = to + mask[own, names[slot]]
-                return to
-
-            end = lax.fori_loop(0, blocks // 8, col, base)
-            count = end - base
-            keep = which[base]
-            for extra in range(SLOTS):
-                which[end + extra] = keep
+            start = qi * span
+            count = ends[qi] - start
             items = lax.div(count + (SLOTS - 1), SLOTS)
 
             def mark(t, left):
                 who[item + t] = qi - part * size
+                where[item + t] = start + t * SLOTS
                 valid[item + t] = left
                 first[item + t] = 0
                 return left - SLOTS
@@ -140,21 +153,19 @@
             last = start + jnp.maximum(load[s] - 1, 0)
             idle = load[s] == 0
             qi = jnp.where(idle, size, who[last])
-            key = jnp.where(idle, 0, which[last * SLOTS])
+            key = jnp.where(idle, 0, where[last])
 
             def fill(t, _):
-                at = start + t
-                who[at] = qi
-                valid[at] = 0
-                first[at] = 0
-                for e in range(SLOTS):
-                    which[at * SLOTS + e] = key
+                who[start + t] = qi
+                where[start + t] = key
+                valid[start + t] = 0
+                first[start + t] = 0
                 return 0
 
             lax.fori_loop(load[s], most + 2, fill, 0)
 
 
-def attend_kernel(part, per, cap, n_kv, spans, who, which, valid, first, steps, *rest):
+def attend_kernel(part, per, cap, n_kv, spans, who, where, which, valid, first, steps, *rest):
     ins, rest = rest[:n_kv], rest[n_kv:]
     q_in, rest = rest[: len(spans)], rest[len(spans) :]
     outs, rest = rest[: len(spans)], rest[len(spans) :]
@@ -184,7 +195,8 @@
     acc_s[...] = jnp.zeros(acc_s.shape, jnp.float32)
 
     def keys(s, t):
-        return [which[((part * STREAMS + s) * cap + t) * SLOTS + e] for e in range(SLOTS)]
+        start = where[(part * STREAMS + s) * cap + t]
+        return [which[start + e] for e in range(SLOTS)]
 
     def score(t, buf):
         for s in range(STREAMS):
@@ -249,11 +261,13 @@
             ).astype(jnp.bfloat16)
 
 
-def out_kernel(inner, heads, groups, *refs):
+def out_kernel(inner, heads, groups, other, *refs):
     pieces = [refs[g * heads : (g + 1) * heads] for g in range(groups)]
     ws = refs[groups * heads : groups * heads + groups]
     out = refs[-1]
     a = lax.axis_index("ctx") // inner
+    side = (lax.axis_index("head") % 2) ^ other
+    cols = pl.ds(pl.multiple_of(side * out.shape[1], LANES), out.shape[1])
     half = pieces[0][0].shape[0]
     low = low_half((half, LANES))
     tops, bottoms, rows = [], [], []
@@ -265,7 +279,7 @@
             bottoms.append(jnp.where(low, swap_halves(p0), p1).astype(jnp.bfloat16))
             for e in (0, 1):
                 start = pl.multiple_of(HEAD_DIM * (a ^ (k + e)), HEAD_DIM)
-                rows.append(ws[g][pl.ds(start, HEAD_DIM), :])
+                rows.append(ws[g][pl.ds(start, HEAD_DIM), cols])
     w = jnp.concatenate(rows, axis=0)
     for n, parts in enumerate((tops, bottoms)):
         x = jnp.concatenate(parts, axis=1)
@@ -337,22 +351,27 @@
             functools.partial(list_kernel, inner, heads, per, cap, parts),
             out_shape=[
                 jax.ShapeDtypeStruct((parts * STREAMS * cap,), jnp.int32),
-                jax.ShapeDtypeStruct((parts * STREAMS * cap * SLOTS,), jnp.int32),
+                jax.ShapeDtypeStruct((parts * STREAMS * cap,), jnp.int32),
+                jax.ShapeDtypeStruct((nq * (nb + SLOTS),), jnp.int32),
                 jax.ShapeDtypeStruct((parts * STREAMS * cap,), jnp.int32),
                 jax.ShapeDtypeStruct((parts * STREAMS * cap,), jnp.int32),
                 jax.ShapeDtypeStruct((parts,), jnp.int32),
             ],
             in_specs=[SMEM] * 2,
-            out_specs=[SMEM] * 5,
-            scratch_shapes=[pltpu.SMEM((nb,), jnp.int32), pltpu.SMEM((STREAMS,), jnp.int32)],
+            out_specs=[SMEM] * 6,
+            scratch_shapes=[
+                pltpu.SMEM((nb,), jnp.int32),
+                pltpu.SMEM((nq,), jnp.int32),
+                pltpu.SMEM((STREAMS,), jnp.int32),
+            ],
             name="block_lists",
         )(block_mask, block_order)
         h = lax.axis_index("head")
         w_out, msgs = lax.optimization_barrier((w_out, msgs))
         w_cols = []
-        for j in range(groups):
-            part = lax.dynamic_slice_in_dim(w_out, (h ^ j) * cols, cols, axis=1)
-            w_cols.append(head_swap(part, j))
+        for g in range(0, groups, 2):
+            part = lax.dynamic_slice_in_dim(w_out, (h // 2 ^ g // 2) * 2 * cols, 2 * cols, axis=1)
+            w_cols.append(head_swap(part, g))
         got[0], tables, w_cols = lax.optimization_barrier((got[0], tables, w_cols))
         kv = [spread(got[j], e) for j in range(heads) for e in range(inner)]
         o = []
@@ -369,7 +388,7 @@
             made = pl.pallas_call(
                 functools.partial(attend_kernel, part, per, cap, len(kv), spans),
                 out_shape=[jax.ShapeDtypeStruct((half, LANES), bf)] * near + extra,
-                in_specs=[SMEM] * 5 + [VMEM] * (len(kv) + near),
+                in_specs=[SMEM] * 6 + [VMEM] * (len(kv) + near),
                 out_specs=[VMEM] * (near + len(extra)),
                 scratch_shapes=[
                     pltpu.VMEM((2, mini, LANES, BLOCK), bf),
@@ -389,23 +408,25 @@
         mine = [None] * heads
         for j in reversed(range(heads)):
             mine[j] = turn(o[j], j)
-        parts = [mine]
-        for g in range(1, groups):
-            part = []
+        pieces = []
+        for g in range(0, groups, 2):
             for j in range(heads):
-                if g % 2:
-                    part.append(head_swap(parts[g - 1][j], 1))
-                else:
-                    part.append(head_swap(mine[j], g))
-            parts.append(part)
-        return pl.pallas_call(
-            functools.partial(out_kernel, inner, heads, groups),
-            out_shape=jax.ShapeDtypeStruct((rows, cols), bf),
-            in_specs=[VMEM] * (groups * heads + groups),
-            out_specs=VMEM,
-            compiler_params=params,
-            name="out_proj",
-        )(*[x for part in parts for x in part], *w_cols)
+                pieces.append(head_swap(mine[j], g))
+
+        def out(other, dtype):
+            return pl.pallas_call(
+                functools.partial(out_kernel, inner, heads, groups // 2, other),
+                out_shape=jax.ShapeDtypeStruct((rows, cols), dtype),
+                in_specs=[VMEM] * (len(pieces) + len(w_cols)),
+                out_specs=VMEM,
+                compiler_params=params,
+                cost_estimate=pl.CostEstimate(
+                    flops=rows * cols * w_out.shape[0] * 4, bytes_accessed=0, transcendentals=0
+                ),
+            )(*pieces, *w_cols)
+
+        theirs = head_swap(out(1, bf), 1)
+        return (out(0, jnp.float32) + theirs.astype(jnp.float32)).astype(bf)
 
     placed = (
         P("ctx", None),

time: 62.1 us -> 54.8 us (0.88)
  starting transfers between devices: 37.7 us -> 31.2 us
  Pallas kernels: 16.3 us -> 15.2 us
  other arithmetic: 0 us -> 0.76 us
    ppermute x15 -> x6, starting transfers between devices: 17.1 us -> 10.6 us  [head_swap(): lax.ppermute(x, 'head', [(h, h ^ j) for h in range(groups)])]
    ppermute x10, starting transfers between devices: 18.7 us -> 13.7 us  [turn(): return lax.ppermute(x, both, pairs)]
    ppermute x4, starting transfers between devices: 1.91 us -> 6.86 us  [spread(): return lax.ppermute(x, both, pairs) if e else x]
    convert_element_type x0 -> x1, other arithmetic: none -> 0.76 us  [body(): return (out(0, jnp.float32) + theirs.astype(jnp.float32)).astype(bf)]
    pallas_call x1, Pallas kernels: 4.54 us -> 3.87 us  [body(): pl.pallas_call(functools.partial(list_kernel, inner, heads, per, cap, par...]
    ppermute x15 -> x6, waiting for transfers between devices: 5.29 us -> 4.72 us  [head_swap(): lax.ppermute(x, 'head', [(h, h ^ j) for h in range(groups)])]
    pallas_call x1 -> x2, Pallas kernels: 1.27 us -> 0.73 us  [out(): pl.pallas_call(functools.partial(out_kernel, inner, heads, groups // 2, o...]
  transfers between devices with their start and end apart: 29 -> 20, of which waited for: 6 -> 7; matrix products, arithmetic and copies ran while one was open for 0% -> 0% of each run, Pallas kernels for 18% -> 20%
where the time goes in v1:
time: 54.8 us; the launch traced here: 54.6 us
  starting transfers between devices  31.2 us (57%)
  Pallas kernels  15.2 us (28%)
  waiting for transfers between devices  7.11 us (13%)
  other arithmetic  0.76 us (1%)
    ppermute x10, starting transfers between devices, turn(): return lax.ppermute(x, both, pairs)  13.7 us
    ppermute x6, starting transfers between devices, head_swap(): lax.ppermute(x, 'head', [(h, h ^ j) for h in range(groups)])  10.6 us
    pallas_call x2, Pallas kernels, body(): pl.pallas_call(functools.partial(attend_kernel, part, per, cap, len(kv),...  6.92 us
    ppermute x4, starting transfers between devices, spread(): return lax.ppermute(x, both, pairs) if e else x  6.86 us
    ppermute x6, waiting for transfers between devices, head_swap(): lax.ppermute(x, 'head', [(h, h ^ j) for h in range(groups)])  4.72 us
    pallas_call x1, Pallas kernels, body(): pl.pallas_call(functools.partial(list_kernel, inner, heads, per, cap, par...  3.87 us
    pallas_call x1, Pallas kernels, body(): pl.pallas_call(functools.partial(proj_kernel, inner, heads, near), out_sh...  3.64 us
    ppermute x10, waiting for transfers between devices, turn(): return lax.ppermute(x, both, pairs)  2.38 us
  transfers between devices with their start and end apart: 20, of which 7 were waited for; matrix products, arithmetic and copies ran while one was open for 0% of the time, Pallas kernels for 20%

profile of v1, /device:TPU:0, one launch (start us, length us, event | category | flops | bytes accessed | tf_op | source)
XLA Modules:
  0.0 54.6 jit_solution(16179485131729856096)
XLA Ops:
  0.0 3.6 %proj.1 = (bf16[768,128]{1,0:T(8,128)(2,1)}, bf16[768,128]{1,0:T(8,128)(2,1)}, bf16[512,128]{1,0:T(8,128)(2,1)}, bf16[512,128]{1,0:T(8,128)(2,1)}, bf16[256,128]{1,0:T(8,128)(2,1)}, /*index=5*/bf16[256,128]{1,0:T(8,128)(2,1)}) custom-call(bf16[512,1024]{1,0:T(8,128)(2,1)} %tok_in.1, bf16[1024,256]{1,0:T(8,128)(2,1)} %wk_in.1, bf16[1024,256]{1,0:T(8,128)(2,1)} %wv_in.1, ...), custom_call_target="tpu_custom_call" | custom-call | tf_op jit(solution)/shard_map/proj/pallas_call | solution.py:329
  3.7 0.0 copy-done.6
  3.7 0.0 copy-start.8
  3.7 0.0 copy-start.7
  3.7 0.0 copy-start.10
  3.7 0.0 copy-start.9
  3.7 0.0 copy-start.12
  3.7 0.0 copy-start.11
  3.8 3.0 %collective-permute-start.1 = (bf16[256,512]{1,0:T(8,128)(2,1)S(1)}, bf16[256,512]{1,0:T(8,128)(2,1)S(1)}, u32[]{:S(2)}, u32[]{:S(2)}) collective-permute-start(bf16[256,512]{1,0:T(8,128)(2,1)S(1)} %get-tuple-element.61), channel_id=1, source_target_pairs={{0,2},{1,3},{2,0},{3,1},{4,6},{5,7},{6,4},{7,5},{8,10},{9,11},{10,... | collective-permute-start | bytes 786440 | tf_op jit(solution)/shard_map/ppermute | solution.py:324
  6.8 0.0 copy-done.8
  6.8 1.6 %collective-permute-start.3 = (bf16[768,128]{1,0:T(8,128)(2,1)S(1)}, bf16[768,128]{1,0:T(8,128)(2,1)S(1)}, u32[]{:S(2)}, u32[]{:S(2)}) collective-permute-start(bf16[768,128]{1,0:T(8,128)(2,1)S(1)} %copy-done.8), channel_id=1, source_target_pairs={{0,8},{1,12},{2,10},{3,14},{4,9},{5,13},{6,11},{7,15},{8,0},{9,4},... | collective-permute-start | bytes 589832 | tf_op jit(solution)/shard_map/ppermute | solution.py:315
  8.4 0.0 copy-done.7
  8.4 0.7 %collective-permute-start = (bf16[768,128]{1,0:T(8,128)(2,1)S(1)}, bf16[768,128]{1,0:T(8,128)(2,1)S(1)}, u32[]{:S(2)}, u32[]{:S(2)}) collective-permute-start(bf16[768,128]{1,0:T(8,128)(2,1)S(1)} %copy-done.7), channel_id=1, source_target_pairs={{0,0},{1,4},{2,2},{3,6},{4,1},{5,5},{6,3},{7,7},{8,8},{9,12},{10,1... | collective-permute-start | bytes 589832 | tf_op jit(solution)/shard_map/ppermute | solution.py:315
  9.1 0.0 copy-done.10
  9.1 2.7 %collective-permute-start.5 = (bf16[512,128]{1,0:T(8,128)(2,1)S(1)}, bf16[512,128]{1,0:T(8,128)(2,1)S(1)}, u32[]{:S(2)}, u32[]{:S(2)}) collective-permute-start(bf16[512,128]{1,0:T(8,128)(2,1)S(1)} %copy-done.10), channel_id=1, source_target_pairs={{0,16},{1,20},{2,18},{3,22},{4,17},{5,21},{6,19},{7,23},{8,24},{9,... | collective-permute-start | bytes 393224 | tf_op jit(solution)/shard_map/ppermute | solution.py:315
  11.7 0.0 copy-done.9
  11.7 0.2 collective-permute-start.7
  12.0 3.9 %block_lists.1 = (s32[216]{0:T(256)}, s32[216]{0:T(256)}, s32[576]{0:T(1024)}, s32[216]{0:T(256)}, s32[216]{0:T(256)}, /*index=5*/s32[2]{0:T(128)}) custom-call(s32[32,32]{1,0:T(8,128)} %mask.1, s32[32]{0:T(128)} %order.1), custom_call_target="tpu_custom_call" | custom-call | tf_op jit(solution)/shard_map/block_lists/pallas_call | solution.py:350
  15.8 0.0 collective-permute-done.3.rest_2_.rest_9_
  15.8 3.3 %collective-permute-start.4 = (bf16[768,128]{1,0:T(8,128)(2,1)S(1)}, bf16[768,128]{1,0:T(8,128)(2,1)S(1)}, u32[]{:S(2)}, u32[]{:S(2)}) collective-permute-start(bf16[768,128]{1,0:T(8,128)(2,1)S(1)} %collective-permute-done.3.rest_2_.rest_9_), channel_id=1, source_target_pairs={{0,1},{1,0},{2,3},{3,2},{4,5},{5,4},{6,7},{7,6},{8,9},{9,8},{10,11... | collective-permute-start | bytes 589832 | tf_op jit(solution)/shard_map/ppermute | solution.py:321
  19.1 0.0 collective-permute-done.rest_0_.rest_8_
  19.1 0.0 collective-permute-done.1.refs_9_
  19.1 0.0 copy-start
  19.1 0.0 copy-start.2
  19.1 0.0 copy-start.3
  19.2 0.0 copy-start.1
  19.2 0.0 copy-start.5
  19.2 0.1 collective-permute-start.2
  19.3 0.0 collective-permute-done.5.rest_4_
  19.3 3.5 %collective-permute-start.6 = (bf16[512,128]{1,0:T(8,128)(2,1)S(1)}, bf16[512,128]{1,0:T(8,128)(2,1)S(1)}, u32[]{:S(2)}, u32[]{:S(2)}) collective-permute-start(bf16[512,128]{1,0:T(8,128)(2,1)S(1)} %collective-permute-done.5.rest_4_), channel_id=1, source_target_pairs={{0,1},{1,0},{2,3},{3,2},{4,5},{5,4},{6,7},{7,6},{8,9},{9,8},{10,11... | collective-permute-start | bytes 393224 | tf_op jit(solution)/shard_map/ppermute | solution.py:321
  22.8 0.0 collective-permute-done.7.rest_6_
  22.8 0.0 collective-permute-start.8
  22.8 0.0 copy-done.12
  22.8 2.8 %collective-permute-start.11 = (bf16[256,128]{1,0:T(8,128)(2,1)S(1)}, bf16[256,128]{1,0:T(8,128)(2,1)S(1)}, u32[]{:S(2)}, u32[]{:S(2)}) collective-permute-start(bf16[256,128]{1,0:T(8,128)(2,1)S(1)} %copy-done.12), channel_id=1, source_target_pairs={{0,16},{1,20},{2,18},{3,22},{4,17},{5,21},{6,19},{7,23},{8,24},{9,... | collective-permute-start | bytes 196616 | tf_op jit(solution)/shard_map/ppermute | solution.py:315
  25.6 0.0 collective-permute-done.6.rest_5_
  25.6 1.5 %collective-permute-start.12 = (bf16[256,128]{1,0:T(8,128)(2,1)S(1)}, bf16[256,128]{1,0:T(8,128)(2,1)S(1)}, u32[]{:S(2)}, u32[]{:S(2)}) collective-permute-start(bf16[256,128]{1,0:T(8,128)(2,1)S(1)} %copy-done.11), channel_id=1, source_target_pairs={{0,24},{1,28},{2,26},{3,30},{4,25},{5,29},{6,27},{7,31},{8,16},{9,... | collective-permute-start | bytes 196616 | tf_op jit(solution)/shard_map/ppermute | solution.py:315
  27.1 0.0 collective-permute-done.8.rest_7_
  27.1 0.0 collective-permute-done.4.rest_3_
  27.1 0.0 collective-permute-done.2.rest_1_
  27.2 3.0 %shard_map.73 = (bf16[256,128]{1,0:T(8,128)(2,1)S(1)}, bf16[256,128]{1,0:T(8,128)(2,1)S(1)}, bf16[16,128,128]{2,1,0:T(8,128)(2,1)S(1)}, bf16[32,64,128]{2,1,0:T(8,128)(2,1)S(1)}) custom-call(s32[216]{0:T(256)S(1)} %copy-done.1, s32[216]{0:T(256)S(1)} %copy-done.2, s32[576]{0:T(1024)S(1)} %copy-done, s32[216]{0:T(256)S(1)} %copy-done.3, s32[216]{0:T(256)S(1)} %copy-done.4, ...), custom_call_target="tpu_custom_call" | custom-call | tf_op jit(solution)/shard_map/pallas_call | solution.py:388
  30.2 0.7 %collective-permute-start.9 = (bf16[256,128]{1,0:T(8,128)(2,1)S(1)}, bf16[256,128]{1,0:T(8,128)(2,1)S(1)}, u32[]{:S(2)}, u32[]{:S(2)}) collective-permute-start(bf16[256,128]{1,0:T(8,128)(2,1)S(1)} %get-tuple-element.53), channel_id=1, source_target_pairs={{0,0},{1,4},{2,2},{3,6},{4,1},{5,5},{6,3},{7,7},{8,8},{9,12},{10,1... | collective-permute-start | bytes 196616 | tf_op jit(solution)/shard_map/ppermute | solution.py:315
  30.9 0.1 collective-permute-start.10
  31.0 0.0 collective-permute-done.11.rest_2_
  31.0 1.3 %collective-permute-done.12.rest_3_ = bf16[256,128]{1,0:T(8,128)(2,1)S(1)} collective-permute-done((bf16[256,128]{1,0:T(8,128)(2,1)S(1)}, bf16[256,128]{1,0:T(8,128)(2,1)S(1)}, u32[]{:S(2)}, u32[]{:S(2)}) %collective-permute-start.12) | collective-permute-done | bytes 65568 | tf_op jit(solution)/shard_map/ppermute | solution.py:315
  32.3 3.9 %shard_map.74 = (bf16[256,128]{1,0:T(8,128)(2,1)S(1)}, bf16[256,128]{1,0:T(8,128)(2,1)S(1)}) custom-call(s32[216]{0:T(256)S(1)} %copy-done.1, s32[216]{0:T(256)S(1)} %copy-done.2, s32[576]{0:T(1024)S(1)} %copy-done, s32[216]{0:T(256)S(1)} %copy-done.3, s32[216]{0:T(256)S(1)} %copy-done.4, s32[2]{0:T(128)S(1)} %copy-done.5, ...), custom_call_target="tpu_custom_call" | custom-call | tf_op jit(solution)/shard_map/pallas_call | solution.py:388
  36.2 1.6 %collective-permute-start.13 = (bf16[256,128]{1,0:T(8,128)(2,1)S(1)}, bf16[256,128]{1,0:T(8,128)(2,1)S(1)}, u32[]{:S(2)}, u32[]{:S(2)}) collective-permute-start(bf16[256,128]{1,0:T(8,128)(2,1)S(1)} %get-tuple-element.57), channel_id=1, source_target_pairs={{0,16},{1,20},{2,18},{3,22},{4,17},{5,21},{6,19},{7,23},{8,24},{9,... | collective-permute-start | bytes 196616 | tf_op jit(solution)/shard_map/ppermute | solution.py:315
  37.8 1.9 %collective-permute-start.14 = (bf16[256,128]{1,0:T(8,128)(2,1)S(1)}, bf16[256,128]{1,0:T(8,128)(2,1)S(1)}, u32[]{:S(2)}, u32[]{:S(2)}) collective-permute-start(bf16[256,128]{1,0:T(8,128)(2,1)S(1)} %get-tuple-element.58), channel_id=1, source_target_pairs={{0,24},{1,28},{2,26},{3,30},{4,25},{5,29},{6,27},{7,31},{8,16},{9,... | collective-permute-start | bytes 196616 | tf_op jit(solution)/shard_map/ppermute | solution.py:315
  39.7 0.0 collective-permute-done.9.refs_0_
  39.7 1.0 %collective-permute-start.15 = (bf16[256,128]{1,0:T(8,128)(2,1)S(1)}, bf16[256,128]{1,0:T(8,128)(2,1)S(1)}, u32[]{:S(2)}, u32[]{:S(2)}) collective-permute-start(bf16[256,128]{1,0:T(8,128)(2,1)S(1)} %collective-permute-done.9.refs_0_), channel_id=1, source_target_pairs={{0,2},{1,3},{2,0},{3,1},{4,6},{5,7},{6,4},{7,5},{8,10},{9,11},{10,... | collective-permute-start | bytes 196616 | tf_op jit(solution)/shard_map/ppermute | solution.py:324
  40.7 0.0 collective-permute-done.10.refs_1_
  40.8 1.0 %collective-permute-start.16 = (bf16[256,128]{1,0:T(8,128)(2,1)S(1)}, bf16[256,128]{1,0:T(8,128)(2,1)S(1)}, u32[]{:S(2)}, u32[]{:S(2)}) collective-permute-start(bf16[256,128]{1,0:T(8,128)(2,1)S(1)} %collective-permute-done.10.refs_1_), channel_id=1, source_target_pairs={{0,2},{1,3},{2,0},{3,1},{4,6},{5,7},{6,4},{7,5},{8,10},{9,11},{10,... | collective-permute-start | bytes 196616 | tf_op jit(solution)/shard_map/ppermute | solution.py:324
  41.7 0.4 collective-permute-done.13.refs_2_
  42.1 1.1 %collective-permute-start.17 = (bf16[256,128]{1,0:T(8,128)(2,1)S(1)}, bf16[256,128]{1,0:T(8,128)(2,1)S(1)}, u32[]{:S(2)}, u32[]{:S(2)}) collective-permute-start(bf16[256,128]{1,0:T(8,128)(2,1)S(1)} %collective-permute-done.13.refs_2_), channel_id=1, source_target_pairs={{0,2},{1,3},{2,0},{3,1},{4,6},{5,7},{6,4},{7,5},{8,10},{9,11},{10,... | collective-permute-start | bytes 196616 | tf_op jit(solution)/shard_map/ppermute | solution.py:324
  43.2 0.7 %collective-permute-done.14.refs_3_ = bf16[256,128]{1,0:T(8,128)(2,1)S(1)} collective-permute-done((bf16[256,128]{1,0:T(8,128)(2,1)S(1)}, bf16[256,128]{1,0:T(8,128)(2,1)S(1)}, u32[]{:S(2)}, u32[]{:S(2)}) %collective-permute-start.14) | collective-permute-done | bytes 65568 | tf_op jit(solution)/shard_map/ppermute | solution.py:315
  43.9 1.0 %collective-permute-start.18 = (bf16[256,128]{1,0:T(8,128)(2,1)S(1)}, bf16[256,128]{1,0:T(8,128)(2,1)S(1)}, u32[]{:S(2)}, u32[]{:S(2)}) collective-permute-start(bf16[256,128]{1,0:T(8,128)(2,1)S(1)} %collective-permute-done.14.refs_3_), channel_id=1, source_target_pairs={{0,2},{1,3},{2,0},{3,1},{4,6},{5,7},{6,4},{7,5},{8,10},{9,11},{10,... | collective-permute-start | bytes 196616 | tf_op jit(solution)/shard_map/ppermute | solution.py:324
  44.9 0.0 collective-permute-done.15.refs_4_
  45.0 0.1 collective-permute-done.16.refs_5_
  45.0 1.4 %collective-permute-done.17.refs_6_ = bf16[256,128]{1,0:T(8,128)(2,1)S(1)} collective-permute-done((bf16[256,128]{1,0:T(8,128)(2,1)S(1)}, bf16[256,128]{1,0:T(8,128)(2,1)S(1)}, u32[]{:S(2)}, u32[]{:S(2)}) %collective-permute-start.17) | collective-permute-done | bytes 65568 | tf_op jit(solution)/shard_map/ppermute | solution.py:324
  46.5 2.4 %collective-permute-done.18.refs_7_ = bf16[256,128]{1,0:T(8,128)(2,1)S(1)} collective-permute-done((bf16[256,128]{1,0:T(8,128)(2,1)S(1)}, bf16[256,128]{1,0:T(8,128)(2,1)S(1)}, u32[]{:S(2)}, u32[]{:S(2)}) %collective-permute-start.18) | collective-permute-done | bytes 65568 | tf_op jit(solution)/shard_map/ppermute | solution.py:324
  48.9 0.4 shard_map.76
  49.2 3.4 %collective-permute-start.19 = (bf16[512,256]{1,0:T(8,128)(2,1)S(1)}, bf16[512,256]{1,0:T(8,128)(2,1)S(1)}, u32[]{:S(2)}, u32[]{:S(2)}) collective-permute-start(bf16[512,256]{1,0:T(8,128)(2,1)S(1)} %shard_map.76), channel_id=1, source_target_pairs={{0,1},{1,0},{2,3},{3,2},{4,5},{5,4},{6,7},{7,6},{8,9},{9,8},{10,11... | collective-permute-start | bytes 786440 | tf_op jit(solution)/shard_map/ppermute | solution.py:324
  52.7 0.4 shard_map.75
  53.0 0.8 %collective-permute-done.19 = bf16[512,256]{1,0:T(8,128)(2,1)S(1)} collective-permute-done((bf16[512,256]{1,0:T(8,128)(2,1)S(1)}, bf16[512,256]{1,0:T(8,128)(2,1)S(1)}, u32[]{:S(2)}, u32[]{:S(2)}) %collective-permute-start.19) | collective-permute-done | bytes 262176 | tf_op jit(solution)/shard_map/ppermute | solution.py:324
  53.8 0.8 %add_convert_fusion = bf16[512,256]{1,0:T(8,128)(2,1)} fusion(f32[512,256]{1,0:T(8,128)S(1)} %shard_map.75, bf16[512,256]{1,0:T(8,128)(2,1)S(1)} %collective-permute-done.19), kind=kLoop, calls=%fused_computation | loop fusion | flops 393216 | bytes 1048576 | tf_op jit(solution)/shard_map/convert_element_type | solution.py:429
  (10 shorter events, 0.1 us)
Async XLA Ops:
  0.0 3.7 %copy-start.6 = (bf16[256,1024]{1,0:T(8,128)(2,1)S(1)}, bf16[256,1024]{1,0:T(8,128)(2,1)}, u32[]{:S(2)}) copy-start(bf16[256,1024]{1,0:T(8,128)(2,1)} %param.11) | copy-start | bytes 1572868
  3.7 3.1 %copy-start.8 = (bf16[768,128]{1,0:T(8,128)(2,1)S(1)}, bf16[768,128]{1,0:T(8,128)(2,1)}, u32[]{:S(2)}) copy-start(bf16[768,128]{1,0:T(8,128)(2,1)} %get-tuple-element.40) | copy-start | bytes 589828
  3.7 4.7 %copy-start.7 = (bf16[768,128]{1,0:T(8,128)(2,1)S(1)}, bf16[768,128]{1,0:T(8,128)(2,1)}, u32[]{:S(2)}) copy-start(bf16[768,128]{1,0:T(8,128)(2,1)} %get-tuple-element.33) | copy-start | bytes 589828
  3.7 5.4 %copy-start.10 = (bf16[512,128]{1,0:T(8,128)(2,1)S(1)}, bf16[512,128]{1,0:T(8,128)(2,1)}, u32[]{:S(2)}) copy-start(bf16[512,128]{1,0:T(8,128)(2,1)} %get-tuple-element.41) | copy-start | bytes 393220
  3.7 8.0 %copy-start.9 = (bf16[512,128]{1,0:T(8,128)(2,1)S(1)}, bf16[512,128]{1,0:T(8,128)(2,1)}, u32[]{:S(2)}) copy-start(bf16[512,128]{1,0:T(8,128)(2,1)} %get-tuple-element.42) | copy-start | bytes 393220
  3.7 19.1 %copy-start.12 = (bf16[256,128]{1,0:T(8,128)(2,1)S(1)}, bf16[256,128]{1,0:T(8,128)(2,1)}, u32[]{:S(2)}) copy-start(bf16[256,128]{1,0:T(8,128)(2,1)} %get-tuple-element.43) | copy-start | bytes 196612
  3.7 21.9 %copy-start.11 = (bf16[256,128]{1,0:T(8,128)(2,1)S(1)}, bf16[256,128]{1,0:T(8,128)(2,1)}, u32[]{:S(2)}) copy-start(bf16[256,128]{1,0:T(8,128)(2,1)} %get-tuple-element.44) | copy-start | bytes 196612
  3.8 15.3 %collective-permute-start.1 = (bf16[256,512]{1,0:T(8,128)(2,1)S(1)}, bf16[256,512]{1,0:T(8,128)(2,1)S(1)}, u32[]{:S(2)}, u32[]{:S(2)}) collective-permute-start(bf16[256,512]{1,0:T(8,128)(2,1)S(1)} %get-tuple-element.61), channel_id=1, source_target_pairs={{0,2},{1,3},{2,0},{3,1},{4,6},{5,7},{6,4},{7,5},{8,10},{9,11},{10,... | collective-permute-start | bytes 786440 | tf_op jit(solution)/shard_map/ppermute | solution.py:324
  6.8 9.0 %collective-permute-start.3 = (bf16[768,128]{1,0:T(8,128)(2,1)S(1)}, bf16[768,128]{1,0:T(8,128)(2,1)S(1)}, u32[]{:S(2)}, u32[]{:S(2)}) collective-permute-start(bf16[768,128]{1,0:T(8,128)(2,1)S(1)} %copy-done.8), channel_id=1, source_target_pairs={{0,8},{1,12},{2,10},{3,14},{4,9},{5,13},{6,11},{7,15},{8,0},{9,4},... | collective-permute-start | bytes 589832 | tf_op jit(solution)/shard_map/ppermute | solution.py:315
  8.4 10.7 %collective-permute-start = (bf16[768,128]{1,0:T(8,128)(2,1)S(1)}, bf16[768,128]{1,0:T(8,128)(2,1)S(1)}, u32[]{:S(2)}, u32[]{:S(2)}) collective-permute-start(bf16[768,128]{1,0:T(8,128)(2,1)S(1)} %copy-done.7), channel_id=1, source_target_pairs={{0,0},{1,4},{2,2},{3,6},{4,1},{5,5},{6,3},{7,7},{8,8},{9,12},{10,1... | collective-permute-start | bytes 589832 | tf_op jit(solution)/shard_map/ppermute | solution.py:315
  9.1 10.2 %collective-permute-start.5 = (bf16[512,128]{1,0:T(8,128)(2,1)S(1)}, bf16[512,128]{1,0:T(8,128)(2,1)S(1)}, u32[]{:S(2)}, u32[]{:S(2)}) collective-permute-start(bf16[512,128]{1,0:T(8,128)(2,1)S(1)} %copy-done.10), channel_id=1, source_target_pairs={{0,16},{1,20},{2,18},{3,22},{4,17},{5,21},{6,19},{7,23},{8,24},{9,... | collective-permute-start | bytes 393224 | tf_op jit(solution)/shard_map/ppermute | solution.py:315
  11.7 11.0 %collective-permute-start.7 = (bf16[512,128]{1,0:T(8,128)(2,1)S(1)}, bf16[512,128]{1,0:T(8,128)(2,1)S(1)}, u32[]{:S(2)}, u32[]{:S(2)}) collective-permute-start(bf16[512,128]{1,0:T(8,128)(2,1)S(1)} %copy-done.9), channel_id=1, source_target_pairs={{0,24},{1,28},{2,26},{3,30},{4,25},{5,29},{6,27},{7,31},{8,16},{9,... | collective-permute-start | bytes 393224 | tf_op jit(solution)/shard_map/ppermute | solution.py:315
  15.8 11.3 %collective-permute-start.4 = (bf16[768,128]{1,0:T(8,128)(2,1)S(1)}, bf16[768,128]{1,0:T(8,128)(2,1)S(1)}, u32[]{:S(2)}, u32[]{:S(2)}) collective-permute-start(bf16[768,128]{1,0:T(8,128)(2,1)S(1)} %collective-permute-done.3.rest_2_.rest_9_), channel_id=1, source_target_pairs={{0,1},{1,0},{2,3},{3,2},{4,5},{5,4},{6,7},{7,6},{8,9},{9,8},{10,11... | collective-permute-start | bytes 589832 | tf_op jit(solution)/shard_map/ppermute | solution.py:321
  19.1 8.0 %copy-start.4 = (s32[216]{0:T(256)S(1)}, s32[216]{0:T(256)}, u32[]{:S(2)}) copy-start(s32[216]{0:T(256)} %get-tuple-element.50.first) | copy-start | bytes 2596
  19.1 8.0 %copy-start = (s32[576]{0:T(1024)S(1)}, s32[576]{0:T(1024)}, u32[]{:S(2)}) copy-start(s32[576]{0:T(1024)} %get-tuple-element.48.which) | copy-start | bytes 6916
  19.1 8.0 %copy-start.2 = (s32[216]{0:T(256)S(1)}, s32[216]{0:T(256)}, u32[]{:S(2)}) copy-start(s32[216]{0:T(256)} %get-tuple-element.47.where) | copy-start | bytes 2596
  19.1 8.0 %copy-start.3 = (s32[216]{0:T(256)S(1)}, s32[216]{0:T(256)}, u32[]{:S(2)}) copy-start(s32[216]{0:T(256)} %get-tuple-element.49.valid) | copy-start | bytes 2596
  19.2 8.0 %copy-start.1 = (s32[216]{0:T(256)S(1)}, s32[216]{0:T(256)}, u32[]{:S(2)}) copy-start(s32[216]{0:T(256)} %get-tuple-element.46.who) | copy-start | bytes 2596
  19.2 8.0 %copy-start.5 = (s32[2]{0:T(128)S(1)}, s32[2]{0:T(128)}, u32[]{:S(2)}) copy-start(s32[2]{0:T(128)} %get-tuple-element.51.steps) | copy-start | bytes 28
  19.2 7.9 %collective-permute-start.2 = (bf16[768,128]{1,0:T(8,128)(2,1)S(1)}, bf16[768,128]{1,0:T(8,128)(2,1)S(1)}, u32[]{:S(2)}, u32[]{:S(2)}) collective-permute-start(bf16[768,128]{1,0:T(8,128)(2,1)S(1)} %collective-permute-done.rest_0_.rest_8_), channel_id=1, source_target_pairs={{0,1},{1,0},{2,3},{3,2},{4,5},{5,4},{6,7},{7,6},{8,9},{9,8},{10,11... | collective-permute-start | bytes 589832 | tf_op jit(solution)/shard_map/ppermute | solution.py:321
  19.3 6.3 %collective-permute-start.6 = (bf16[512,128]{1,0:T(8,128)(2,1)S(1)}, bf16[512,128]{1,0:T(8,128)(2,1)S(1)}, u32[]{:S(2)}, u32[]{:S(2)}) collective-permute-start(bf16[512,128]{1,0:T(8,128)(2,1)S(1)} %collective-permute-done.5.rest_4_), channel_id=1, source_target_pairs={{0,1},{1,0},{2,3},{3,2},{4,5},{5,4},{6,7},{7,6},{8,9},{9,8},{10,11... | collective-permute-start | bytes 393224 | tf_op jit(solution)/shard_map/ppermute | solution.py:321
  22.8 4.3 %collective-permute-start.8 = (bf16[512,128]{1,0:T(8,128)(2,1)S(1)}, bf16[512,128]{1,0:T(8,128)(2,1)S(1)}, u32[]{:S(2)}, u32[]{:S(2)}) collective-permute-start(bf16[512,128]{1,0:T(8,128)(2,1)S(1)} %collective-permute-done.7.rest_6_), channel_id=1, source_target_pairs={{0,1},{1,0},{2,3},{3,2},{4,5},{5,4},{6,7},{7,6},{8,9},{9,8},{10,11... | collective-permute-start | bytes 393224 | tf_op jit(solution)/shard_map/ppermute | solution.py:321
  22.8 8.2 %collective-permute-start.11 = (bf16[256,128]{1,0:T(8,128)(2,1)S(1)}, bf16[256,128]{1,0:T(8,128)(2,1)S(1)}, u32[]{:S(2)}, u32[]{:S(2)}) collective-permute-start(bf16[256,128]{1,0:T(8,128)(2,1)S(1)} %copy-done.12), channel_id=1, source_target_pairs={{0,16},{1,20},{2,18},{3,22},{4,17},{5,21},{6,19},{7,23},{8,24},{9,... | collective-permute-start | bytes 196616 | tf_op jit(solution)/shard_map/ppermute | solution.py:315
  25.6 6.7 %collective-permute-start.12 = (bf16[256,128]{1,0:T(8,128)(2,1)S(1)}, bf16[256,128]{1,0:T(8,128)(2,1)S(1)}, u32[]{:S(2)}, u32[]{:S(2)}) collective-permute-start(bf16[256,128]{1,0:T(8,128)(2,1)S(1)} %copy-done.11), channel_id=1, source_target_pairs={{0,24},{1,28},{2,26},{3,30},{4,25},{5,29},{6,27},{7,31},{8,16},{9,... | collective-permute-start | bytes 196616 | tf_op jit(solution)/shard_map/ppermute | solution.py:315
  30.2 9.5 %collective-permute-start.9 = (bf16[256,128]{1,0:T(8,128)(2,1)S(1)}, bf16[256,128]{1,0:T(8,128)(2,1)S(1)}, u32[]{:S(2)}, u32[]{:S(2)}) collective-permute-start(bf16[256,128]{1,0:T(8,128)(2,1)S(1)} %get-tuple-element.53), channel_id=1, source_target_pairs={{0,0},{1,4},{2,2},{3,6},{4,1},{5,5},{6,3},{7,7},{8,8},{9,12},{10,1... | collective-permute-start | bytes 196616 | tf_op jit(solution)/shard_map/ppermute | solution.py:315
  30.9 9.9 %collective-permute-start.10 = (bf16[256,128]{1,0:T(8,128)(2,1)S(1)}, bf16[256,128]{1,0:T(8,128)(2,1)S(1)}, u32[]{:S(2)}, u32[]{:S(2)}) collective-permute-start(bf16[256,128]{1,0:T(8,128)(2,1)S(1)} %get-tuple-element.54), channel_id=1, source_target_pairs={{0,8},{1,12},{2,10},{3,14},{4,9},{5,13},{6,11},{7,15},{8,0},{9,4},... | collective-permute-start | bytes 196616 | tf_op jit(solution)/shard_map/ppermute | solution.py:315
  36.2 5.9 %collective-permute-start.13 = (bf16[256,128]{1,0:T(8,128)(2,1)S(1)}, bf16[256,128]{1,0:T(8,128)(2,1)S(1)}, u32[]{:S(2)}, u32[]{:S(2)}) collective-permute-start(bf16[256,128]{1,0:T(8,128)(2,1)S(1)} %get-tuple-element.57), channel_id=1, source_target_pairs={{0,16},{1,20},{2,18},{3,22},{4,17},{5,21},{6,19},{7,23},{8,24},{9,... | collective-permute-start | bytes 196616 | tf_op jit(solution)/shard_map/ppermute | solution.py:315
  37.8 6.1 %collective-permute-start.14 = (bf16[256,128]{1,0:T(8,128)(2,1)S(1)}, bf16[256,128]{1,0:T(8,128)(2,1)S(1)}, u32[]{:S(2)}, u32[]{:S(2)}) collective-permute-start(bf16[256,128]{1,0:T(8,128)(2,1)S(1)} %get-tuple-element.58), channel_id=1, source_target_pairs={{0,24},{1,28},{2,26},{3,30},{4,25},{5,29},{6,27},{7,31},{8,16},{9,... | collective-permute-start | bytes 196616 | tf_op jit(solution)/shard_map/ppermute | solution.py:315
  39.7 5.2 %collective-permute-start.15 = (bf16[256,128]{1,0:T(8,128)(2,1)S(1)}, bf16[256,128]{1,0:T(8,128)(2,1)S(1)}, u32[]{:S(2)}, u32[]{:S(2)}) collective-permute-start(bf16[256,128]{1,0:T(8,128)(2,1)S(1)} %collective-permute-done.9.refs_0_), channel_id=1, source_target_pairs={{0,2},{1,3},{2,0},{3,1},{4,6},{5,7},{6,4},{7,5},{8,10},{9,11},{10,... | collective-permute-start | bytes 196616 | tf_op jit(solution)/shard_map/ppermute | solution.py:324
  40.8 4.3 %collective-permute-start.16 = (bf16[256,128]{1,0:T(8,128)(2,1)S(1)}, bf16[256,128]{1,0:T(8,128)(2,1)S(1)}, u32[]{:S(2)}, u32[]{:S(2)}) collective-permute-start(bf16[256,128]{1,0:T(8,128)(2,1)S(1)} %collective-permute-done.10.refs_1_), channel_id=1, source_target_pairs={{0,2},{1,3},{2,0},{3,1},{4,6},{5,7},{6,4},{7,5},{8,10},{9,11},{10,... | collective-permute-start | bytes 196616 | tf_op jit(solution)/shard_map/ppermute | solution.py:324
  42.1 4.4 %collective-permute-start.17 = (bf16[256,128]{1,0:T(8,128)(2,1)S(1)}, bf16[256,128]{1,0:T(8,128)(2,1)S(1)}, u32[]{:S(2)}, u32[]{:S(2)}) collective-permute-start(bf16[256,128]{1,0:T(8,128)(2,1)S(1)} %collective-permute-done.13.refs_2_), channel_id=1, source_target_pairs={{0,2},{1,3},{2,0},{3,1},{4,6},{5,7},{6,4},{7,5},{8,10},{9,11},{10,... | collective-permute-start | bytes 196616 | tf_op jit(solution)/shard_map/ppermute | solution.py:324
  43.9 5.0 %collective-permute-start.18 = (bf16[256,128]{1,0:T(8,128)(2,1)S(1)}, bf16[256,128]{1,0:T(8,128)(2,1)S(1)}, u32[]{:S(2)}, u32[]{:S(2)}) collective-permute-start(bf16[256,128]{1,0:T(8,128)(2,1)S(1)} %collective-permute-done.14.refs_3_), channel_id=1, source_target_pairs={{0,2},{1,3},{2,0},{3,1},{4,6},{5,7},{6,4},{7,5},{8,10},{9,11},{10,... | collective-permute-start | bytes 196616 | tf_op jit(solution)/shard_map/ppermute | solution.py:324
  49.2 4.6 %collective-permute-start.19 = (bf16[512,256]{1,0:T(8,128)(2,1)S(1)}, bf16[512,256]{1,0:T(8,128)(2,1)S(1)}, u32[]{:S(2)}, u32[]{:S(2)}) collective-permute-start(bf16[512,256]{1,0:T(8,128)(2,1)S(1)} %shard_map.76), channel_id=1, source_target_pairs={{0,1},{1,0},{2,3},{3,2},{4,5},{5,4},{6,7},{7,6},{8,9},{9,8},{10,11... | collective-permute-start | bytes 786440 | tf_op jit(solution)/shard_map/ppermute | solution.py:324

commit v2 on v1

--- a/solution.py
+++ b/solution.py
@@ -241,6 +241,7 @@
             l_all[qi] = total
 
     score(0, 0)
+    count = steps[part]
 
     def step(u, _):
         t = 2 * u
@@ -250,7 +251,12 @@
         weigh(t + 1, 1)
         return 0
 
-    lax.fori_loop(0, lax.div(steps[part] + 1, 2), step, 0)
+    lax.fori_loop(0, lax.div(count, 2), step, 0)
+
+    @pl.when(lax.rem(count, 2) == 1)
+    def _():
+        weigh(count - 1, 0)
+
     for k in range(len(spans)):
         for r in range(half):
             done = []
@@ -283,9 +289,10 @@
     w = jnp.concatenate(rows, axis=0)
     for n, parts in enumerate((tops, bottoms)):
         x = jnp.concatenate(parts, axis=1)
-        out[n * half : (n + 1) * half, :] = jnp.dot(
-            x, w, preferred_element_type=jnp.float32
-        ).astype(out.dtype)
+        total = jnp.dot(x, w, preferred_element_type=jnp.float32)
+        if not other:
+            total = total + refs[-2][n * half : (n + 1) * half, :].astype(jnp.float32)
+        out[n * half : (n + 1) * half, :] = total.astype(out.dtype)
 
 
 def solution(mesh):
@@ -342,8 +349,6 @@
         got, late = [None] * heads, [None] * heads
         for j in reversed(range(heads)):
             got[j] = turn(msgs[j], j)
-        for j in range(near, heads):
-            late[j] = turn(msgs[heads + j - near], j)
         parts = heads // near
         longest = -(-nb // SLOTS)
         cap = -(-nq // parts * longest // STREAMS) + longest + 3
@@ -366,14 +371,14 @@
             ],
             name="block_lists",
         )(block_mask, block_order)
-        h = lax.axis_index("head")
-        w_out, msgs = lax.optimization_barrier((w_out, msgs))
-        w_cols = []
-        for g in range(0, groups, 2):
-            part = lax.dynamic_slice_in_dim(w_out, (h // 2 ^ g // 2) * 2 * cols, 2 * cols, axis=1)
-            w_cols.append(head_swap(part, g))
-        got[0], tables, w_cols = lax.optimization_barrier((got[0], tables, w_cols))
-        kv = [spread(got[j], e) for j in range(heads) for e in range(inner)]
+        queries = list(msgs[heads:])
+        queries, got[0], tables = lax.optimization_barrier((queries, got[0], tables))
+        for j in range(near, heads):
+            late[j] = turn(queries[j - near], j)
+        kv = []
+        for j in range(heads):
+            for e in range(inner):
+                kv.append(spread(got[j], e))
         o = []
         for part in range(parts):
             if part == 0:
@@ -404,7 +409,13 @@
             )(*tables, *kv, *queries)
             o += made[:near]
             if part == 0:
-                kv = made[near:]
+                h = lax.axis_index("head")
+                w_out, kv = lax.optimization_barrier((w_out, made[near:]))
+                w_cols = []
+                for g in range(0, groups, 2):
+                    start = (h // 2 ^ g // 2) * 2 * cols
+                    share = lax.dynamic_slice_in_dim(w_out, start, 2 * cols, axis=1)
+                    w_cols.append(head_swap(share, g))
         mine = [None] * heads
         for j in reversed(range(heads)):
             mine[j] = turn(o[j], j)
@@ -413,20 +424,16 @@
             for j in range(heads):
                 pieces.append(head_swap(mine[j], g))
 
-        def out(other, dtype):
+        def out(other, *more):
             return pl.pallas_call(
                 functools.partial(out_kernel, inner, heads, groups // 2, other),
-                out_shape=jax.ShapeDtypeStruct((rows, cols), dtype),
-                in_specs=[VMEM] * (len(pieces) + len(w_cols)),
+                out_shape=jax.ShapeDtypeStruct((rows, cols), bf),
+                in_specs=[VMEM] * (len(pieces) + len(w_cols) + len(more)),
                 out_specs=VMEM,
                 compiler_params=params,
-                cost_estimate=pl.CostEstimate(
-                    flops=rows * cols * w_out.shape[0] * 4, bytes_accessed=0, transcendentals=0
-                ),
-            )(*pieces, *w_cols)
-
-        theirs = head_swap(out(1, bf), 1)
-        return (out(0, jnp.float32) + theirs.astype(jnp.float32)).astype(bf)
+            )(*pieces, *w_cols, *more)
+
+        return out(0, head_swap(out(1), 1))
 
     placed = (
         P("ctx", None),

time: 54.8 us -> 61.8 us (1.13)
  waiting for transfers between devices: 7.11 us -> 14.3 us
  other arithmetic: 0.76 us -> 0 us
    ppermute x10, waiting for transfers between devices: 2.38 us -> 6.54 us  [turn(): return lax.ppermute(x, both, pairs)]
    ppermute x6, starting transfers between devices: 10.6 us -> 7.99 us  [head_swap(): lax.ppermute(x, 'head', [(h, h ^ j) for h in range(groups)])]
    ppermute x10, starting transfers between devices: 13.7 us -> 15.8 us  [turn(): return lax.ppermute(x, both, pairs)]
    ppermute x6, waiting for transfers between devices: 4.72 us -> 6.44 us  [head_swap(): lax.ppermute(x, 'head', [(h, h ^ j) for h in range(groups)])]
    ppermute x4, waiting for transfers between devices: 0.01 us -> 1.28 us  [spread(): return lax.ppermute(x, both, pairs) if e else x]
    convert_element_type x1 -> x0, other arithmetic: 0.76 us -> none  [body(): return (out(0, jnp.float32) + theirs.astype(jnp.float32)).astype(bf)]
    pallas_call x2, Pallas kernels: 0.73 us -> 1.45 us  [out(): pl.pallas_call(functools.partial(out_kernel, inner, heads, groups // 2, o...]
  transfers between devices with their start and end apart: 20 -> 20, of which waited for: 7 -> 10; matrix products, arithmetic and copies ran while one was open for 0% -> 0% of each run, Pallas kernels for 20% -> 13%
where the time goes in v2:
time: 61.8 us; the launch traced here: 61.5 us
  starting transfers between devices  31.2 us (50%)
  Pallas kernels  15.8 us (26%)
  waiting for transfers between devices  14.3 us (23%)
    ppermute x10, starting transfers between devices, turn(): return lax.ppermute(x, both, pairs)  15.8 us
    ppermute x6, starting transfers between devices, head_swap(): lax.ppermute(x, 'head', [(h, h ^ j) for h in range(groups)])  7.99 us
    ppermute x4, starting transfers between devices, spread(): return lax.ppermute(x, both, pairs) if e else x  7.38 us
    pallas_call x2, Pallas kernels, body(): pl.pallas_call(functools.partial(attend_kernel, part, per, cap, len(kv),...  6.92 us
    ppermute x10, waiting for transfers between devices, turn(): return lax.ppermute(x, both, pairs)  6.54 us
    ppermute x6, waiting for transfers between devices, head_swap(): lax.ppermute(x, 'head', [(h, h ^ j) for h in range(groups)])  6.44 us
    pallas_call x1, Pallas kernels, body(): pl.pallas_call(functools.partial(list_kernel, inner, heads, per, cap, par...  3.87 us
    pallas_call x1, Pallas kernels, body(): pl.pallas_call(functools.partial(proj_kernel, inner, heads, near), out_sh...  3.59 us
  transfers between devices with their start and end apart: 20, of which 10 were waited for; matrix products, arithmetic and copies ran while one was open for 0% of the time, Pallas kernels for 13%

profile of v2, /device:TPU:0, one launch (start us, length us, event | category | flops | bytes accessed | tf_op | source)
XLA Modules:
  0.0 61.5 jit_solution(15952041849504217491)
XLA Ops:
  0.0 3.6 %proj.1 = (bf16[768,128]{1,0:T(8,128)(2,1)}, bf16[768,128]{1,0:T(8,128)(2,1)}, bf16[512,128]{1,0:T(8,128)(2,1)}, bf16[512,128]{1,0:T(8,128)(2,1)}, bf16[256,128]{1,0:T(8,128)(2,1)}, /*index=5*/bf16[256,128]{1,0:T(8,128)(2,1)}) custom-call(bf16[512,1024]{1,0:T(8,128)(2,1)} %tok_in.1, bf16[1024,256]{1,0:T(8,128)(2,1)} %wk_in.1, bf16[1024,256]{1,0:T(8,128)(2,1)} %wv_in.1, ...), custom_call_target="tpu_custom_call" | custom-call | tf_op jit(solution)/shard_map/proj/pallas_call | solution.py:336
  3.6 1.6 %collective-permute-start = (bf16[768,128]{1,0:T(8,128)(2,1)}, bf16[768,128]{1,0:T(8,128)(2,1)S(1)}, u32[]{:S(2)}, u32[]{:S(2)}) collective-permute-start(bf16[768,128]{1,0:T(8,128)(2,1)} %get-tuple-element.37), channel_id=1, source_target_pairs={{0,0},{1,4},{2,2},{3,6},{4,1},{5,5},{6,3},{7,7},{8,8},{9,12},{10,1... | collective-permute-start | bytes 589832 | tf_op jit(solution)/shard_map/ppermute | solution.py:322
  5.2 3.1 %collective-permute-start.2 = (bf16[768,128]{1,0:T(8,128)(2,1)}, bf16[768,128]{1,0:T(8,128)(2,1)S(1)}, u32[]{:S(2)}, u32[]{:S(2)}) collective-permute-start(bf16[768,128]{1,0:T(8,128)(2,1)} %get-tuple-element.51), channel_id=1, source_target_pairs={{0,8},{1,12},{2,10},{3,14},{4,9},{5,13},{6,11},{7,15},{8,0},{9,4},... | collective-permute-start | bytes 589832 | tf_op jit(solution)/shard_map/ppermute | solution.py:322
  8.2 2.6 %collective-permute-start.4 = (bf16[512,128]{1,0:T(8,128)(2,1)}, bf16[512,128]{1,0:T(8,128)(2,1)S(1)}, u32[]{:S(2)}, u32[]{:S(2)}) collective-permute-start(bf16[512,128]{1,0:T(8,128)(2,1)} %get-tuple-element.52), channel_id=1, source_target_pairs={{0,16},{1,20},{2,18},{3,22},{4,17},{5,21},{6,19},{7,23},{8,24},{9,... | collective-permute-start | bytes 393224 | tf_op jit(solution)/shard_map/ppermute | solution.py:322
  10.8 0.0 collective-permute-start.6
  10.8 3.9 %block_lists.1 = (s32[216]{0:T(256)}, s32[216]{0:T(256)}, s32[576]{0:T(1024)}, s32[216]{0:T(256)}, s32[216]{0:T(256)}, /*index=5*/s32[2]{0:T(128)}) custom-call(s32[32,32]{1,0:T(8,128)} %mask.1, s32[32]{0:T(128)} %order.1), custom_call_target="tpu_custom_call" | custom-call | tf_op jit(solution)/shard_map/block_lists/pallas_call | solution.py:355
  14.7 0.0 collective-permute-done.rest_0_.rest_8_
  14.7 2.6 %collective-permute-start.1 = (bf16[768,128]{1,0:T(8,128)(2,1)S(1)}, bf16[768,128]{1,0:T(8,128)(2,1)S(1)}, u32[]{:S(2)}, u32[]{:S(2)}) collective-permute-start(bf16[768,128]{1,0:T(8,128)(2,1)S(1)} %collective-permute-done.rest_0_.rest_8_), channel_id=1, source_target_pairs={{0,1},{1,0},{2,3},{3,2},{4,5},{5,4},{6,7},{7,6},{8,9},{9,8},{10,11... | collective-permute-start | bytes 589832 | tf_op jit(solution)/shard_map/ppermute | solution.py:328
  17.4 0.0 collective-permute-done.2.rest_2_.rest_9_
  17.4 0.1 collective-permute-start.3
  17.4 0.0 collective-permute-done.4.rest_4_
  17.4 4.7 %collective-permute-start.5 = (bf16[512,128]{1,0:T(8,128)(2,1)S(1)}, bf16[512,128]{1,0:T(8,128)(2,1)S(1)}, u32[]{:S(2)}, u32[]{:S(2)}) collective-permute-start(bf16[512,128]{1,0:T(8,128)(2,1)S(1)} %collective-permute-done.4.rest_4_), channel_id=1, source_target_pairs={{0,1},{1,0},{2,3},{3,2},{4,5},{5,4},{6,7},{7,6},{8,9},{9,8},{10,11... | collective-permute-start | bytes 393224 | tf_op jit(solution)/shard_map/ppermute | solution.py:328
  22.1 0.0 collective-permute-done.6.rest_6_
  22.1 0.0 collective-permute-start.7
  22.1 0.0 copy-start.4
  22.1 0.0 copy-start
  22.1 0.0 copy-start.3
  22.1 0.0 copy-start.5
  22.1 0.0 copy-start.1
  22.2 0.0 copy-start.2
  22.2 0.0 copy-start.6
  22.2 0.9 %collective-permute-done.5.rest_5_ = bf16[512,128]{1,0:T(8,128)(2,1)S(1)} collective-permute-done((bf16[512,128]{1,0:T(8,128)(2,1)S(1)}, bf16[512,128]{1,0:T(8,128)(2,1)S(1)}, u32[]{:S(2)}, u32[]{:S(2)}) %collective-permute-start.5) | collective-permute-done | bytes 131104 | tf_op jit(solution)/shard_map/ppermute | solution.py:328
  23.1 0.4 collective-permute-done.7.rest_7_
  23.5 0.0 collective-permute-done.1.rest_1_
  23.5 0.0 collective-permute-done.3.rest_3_
  23.5 0.0 copy-done.4
  23.5 0.0 copy-done
  23.5 0.0 copy-done.3
  23.5 0.0 copy-done.5
  23.5 0.0 copy-done.1
  23.5 0.0 copy-done.2
  23.5 3.0 %shard_map.73 = (bf16[256,128]{1,0:T(8,128)(2,1)S(1)}, bf16[256,128]{1,0:T(8,128)(2,1)S(1)}, bf16[16,128,128]{2,1,0:T(8,128)(2,1)S(1)}, bf16[32,64,128]{2,1,0:T(8,128)(2,1)S(1)}) custom-call(s32[216]{0:T(256)S(1)} %copy-done.1, s32[216]{0:T(256)S(1)} %copy-done.2, s32[576]{0:T(1024)S(1)} %copy-done, s32[216]{0:T(256)S(1)} %copy-done.3, s32[216]{0:T(256)S(1)} %copy-done.4, ...), custom_call_target="tpu_custom_call" | custom-call | tf_op jit(solution)/shard_map/pallas_call | solution.py:393
  26.6 0.0 copy-done.6
  26.6 0.0 copy-start.8
  26.6 0.0 copy-start.7
  26.7 1.6 %collective-permute-start.18 = (bf16[256,512]{1,0:T(8,128)(2,1)S(1)}, bf16[256,512]{1,0:T(8,128)(2,1)S(1)}, u32[]{:S(2)}, u32[]{:S(2)}) collective-permute-start(bf16[256,512]{1,0:T(8,128)(2,1)S(1)} %get-tuple-element.65), channel_id=1, source_target_pairs={{0,2},{1,3},{2,0},{3,1},{4,6},{5,7},{6,4},{7,5},{8,10},{9,11},{10,... | collective-permute-start | bytes 786440 | tf_op jit(solution)/shard_map/ppermute | solution.py:331
  28.2 0.0 copy-done.8
  28.2 3.6 %collective-permute-start.10 = (bf16[256,128]{1,0:T(8,128)(2,1)S(1)}, bf16[256,128]{1,0:T(8,128)(2,1)S(1)}, u32[]{:S(2)}, u32[]{:S(2)}) collective-permute-start(bf16[256,128]{1,0:T(8,128)(2,1)S(1)} %copy-done.8), channel_id=1, source_target_pairs={{0,16},{1,20},{2,18},{3,22},{4,17},{5,21},{6,19},{7,23},{8,24},{9,... | collective-permute-start | bytes 196616 | tf_op jit(solution)/shard_map/ppermute | solution.py:322
  31.8 0.0 copy-done.7
  31.8 0.4 collective-permute-start.11
  32.2 2.7 %collective-permute-done.10.rest_2_ = bf16[256,128]{1,0:T(8,128)(2,1)S(1)} collective-permute-done((bf16[256,128]{1,0:T(8,128)(2,1)S(1)}, bf16[256,128]{1,0:T(8,128)(2,1)S(1)}, u32[]{:S(2)}, u32[]{:S(2)}) %collective-permute-start.10) | collective-permute-done | bytes 65568 | tf_op jit(solution)/shard_map/ppermute | solution.py:322
  34.9 2.9 %collective-permute-done.11.rest_3_ = bf16[256,128]{1,0:T(8,128)(2,1)S(1)} collective-permute-done((bf16[256,128]{1,0:T(8,128)(2,1)S(1)}, bf16[256,128]{1,0:T(8,128)(2,1)S(1)}, u32[]{:S(2)}, u32[]{:S(2)}) %collective-permute-start.11) | collective-permute-done | bytes 65568 | tf_op jit(solution)/shard_map/ppermute | solution.py:322
  37.8 3.9 %shard_map.74 = (bf16[256,128]{1,0:T(8,128)(2,1)S(1)}, bf16[256,128]{1,0:T(8,128)(2,1)S(1)}) custom-call(s32[216]{0:T(256)S(1)} %copy-done.1, s32[216]{0:T(256)S(1)} %copy-done.2, s32[576]{0:T(1024)S(1)} %copy-done, s32[216]{0:T(256)S(1)} %copy-done.3, s32[216]{0:T(256)S(1)} %copy-done.4, s32[2]{0:T(128)S(1)} %copy-done.5, ...), custom_call_target="tpu_custom_call" | custom-call | tf_op jit(solution)/shard_map/pallas_call | solution.py:393
  41.7 1.0 %collective-permute-start.12 = (bf16[256,128]{1,0:T(8,128)(2,1)S(1)}, bf16[256,128]{1,0:T(8,128)(2,1)S(1)}, u32[]{:S(2)}, u32[]{:S(2)}) collective-permute-start(bf16[256,128]{1,0:T(8,128)(2,1)S(1)} %get-tuple-element.62), channel_id=1, source_target_pairs={{0,16},{1,20},{2,18},{3,22},{4,17},{5,21},{6,19},{7,23},{8,24},{9,... | collective-permute-start | bytes 196616 | tf_op jit(solution)/shard_map/ppermute | solution.py:322
  42.7 2.8 %collective-permute-start.13 = (bf16[256,128]{1,0:T(8,128)(2,1)S(1)}, bf16[256,128]{1,0:T(8,128)(2,1)S(1)}, u32[]{:S(2)}, u32[]{:S(2)}) collective-permute-start(bf16[256,128]{1,0:T(8,128)(2,1)S(1)} %get-tuple-element.63), channel_id=1, source_target_pairs={{0,24},{1,28},{2,26},{3,30},{4,25},{5,29},{6,27},{7,31},{8,16},{9,... | collective-permute-start | bytes 196616 | tf_op jit(solution)/shard_map/ppermute | solution.py:322
  45.6 0.7 %collective-permute-start.8 = (bf16[256,128]{1,0:T(8,128)(2,1)S(1)}, bf16[256,128]{1,0:T(8,128)(2,1)S(1)}, u32[]{:S(2)}, u32[]{:S(2)}) collective-permute-start(bf16[256,128]{1,0:T(8,128)(2,1)S(1)} %get-tuple-element.54), channel_id=1, source_target_pairs={{0,0},{1,4},{2,2},{3,6},{4,1},{5,5},{6,3},{7,7},{8,8},{9,12},{10,1... | collective-permute-start | bytes 196616 | tf_op jit(solution)/shard_map/ppermute | solution.py:322
  46.2 0.1 collective-permute-start.9
  46.3 0.9 %collective-permute-done.12.refs_2_ = bf16[256,128]{1,0:T(8,128)(2,1)S(1)} collective-permute-done((bf16[256,128]{1,0:T(8,128)(2,1)S(1)}, bf16[256,128]{1,0:T(8,128)(2,1)S(1)}, u32[]{:S(2)}, u32[]{:S(2)}) %collective-permute-start.12) | collective-permute-done | bytes 65568 | tf_op jit(solution)/shard_map/ppermute | solution.py:322
  47.2 4.2 %collective-permute-start.16 = (bf16[256,128]{1,0:T(8,128)(2,1)S(1)}, bf16[256,128]{1,0:T(8,128)(2,1)S(1)}, u32[]{:S(2)}, u32[]{:S(2)}) collective-permute-start(bf16[256,128]{1,0:T(8,128)(2,1)S(1)} %collective-permute-done.12.refs_2_), channel_id=1, source_target_pairs={{0,2},{1,3},{2,0},{3,1},{4,6},{5,7},{6,4},{7,5},{8,10},{9,11},{10,... | collective-permute-start | bytes 196616 | tf_op jit(solution)/shard_map/ppermute | solution.py:331
  51.4 0.0 collective-permute-done.13.refs_3_
  51.4 0.0 collective-permute-start.17
  51.4 0.0 collective-permute-done.8.refs_0_
  51.4 2.0 %collective-permute-start.14 = (bf16[256,128]{1,0:T(8,128)(2,1)S(1)}, bf16[256,128]{1,0:T(8,128)(2,1)S(1)}, u32[]{:S(2)}, u32[]{:S(2)}) collective-permute-start(bf16[256,128]{1,0:T(8,128)(2,1)S(1)} %collective-permute-done.8.refs_0_), channel_id=1, source_target_pairs={{0,2},{1,3},{2,0},{3,1},{4,6},{5,7},{6,4},{7,5},{8,10},{9,11},{10,... | collective-permute-start | bytes 196616 | tf_op jit(solution)/shard_map/ppermute | solution.py:331
  53.4 0.0 collective-permute-done.9.refs_1_
  53.4 0.1 collective-permute-start.15
  53.5 0.6 %collective-permute-done.16.refs_6_ = bf16[256,128]{1,0:T(8,128)(2,1)S(1)} collective-permute-done((bf16[256,128]{1,0:T(8,128)(2,1)S(1)}, bf16[256,128]{1,0:T(8,128)(2,1)S(1)}, u32[]{:S(2)}, u32[]{:S(2)}) %collective-permute-start.16) | collective-permute-done | bytes 65568 | tf_op jit(solution)/shard_map/ppermute | solution.py:331
  54.1 2.2 %collective-permute-done.17.refs_7_ = bf16[256,128]{1,0:T(8,128)(2,1)S(1)} collective-permute-done((bf16[256,128]{1,0:T(8,128)(2,1)S(1)}, bf16[256,128]{1,0:T(8,128)(2,1)S(1)}, u32[]{:S(2)}, u32[]{:S(2)}) %collective-permute-start.17) | collective-permute-done | bytes 65568 | tf_op jit(solution)/shard_map/ppermute | solution.py:331
  56.3 0.8 %collective-permute-done.14.refs_4_ = bf16[256,128]{1,0:T(8,128)(2,1)S(1)} collective-permute-done((bf16[256,128]{1,0:T(8,128)(2,1)S(1)}, bf16[256,128]{1,0:T(8,128)(2,1)S(1)}, u32[]{:S(2)}, u32[]{:S(2)}) %collective-permute-start.14) | collective-permute-done | bytes 65568 | tf_op jit(solution)/shard_map/ppermute | solution.py:331
  57.1 1.4 %collective-permute-done.15.refs_5_ = bf16[256,128]{1,0:T(8,128)(2,1)S(1)} collective-permute-done((bf16[256,128]{1,0:T(8,128)(2,1)S(1)}, bf16[256,128]{1,0:T(8,128)(2,1)S(1)}, u32[]{:S(2)}, u32[]{:S(2)}) %collective-permute-start.15) | collective-permute-done | bytes 65568 | tf_op jit(solution)/shard_map/ppermute | solution.py:331
  58.5 0.0 collective-permute-done.18.refs_9_
  58.5 0.4 shard_map.75
  58.9 0.2 collective-permute-start.19
  59.0 1.4 %collective-permute-done.19.refs_10_ = bf16[512,256]{1,0:T(8,128)(2,1)S(1)} collective-permute-done((bf16[512,256]{1,0:T(8,128)(2,1)S(1)}, bf16[512,256]{1,0:T(8,128)(2,1)S(1)}, u32[]{:S(2)}, u32[]{:S(2)}) %collective-permute-start.19) | collective-permute-done | bytes 262176 | tf_op jit(solution)/shard_map/ppermute | solution.py:331
  60.5 1.1 %shard_map.76 = bf16[512,256]{1,0:T(8,128)(2,1)} custom-call(bf16[256,128]{1,0:T(8,128)(2,1)S(1)} %collective-permute-done.8.refs_0_, bf16[256,128]{1,0:T(8,128)(2,1)S(1)} %collective-permute-done.9.refs_1_, bf16[256,128]{1,0:T(8,128)(2,1)S(1)} %collective-permute-done.12.refs_2_, bf16[256,128]{1,0:T(8,128)(2,1)S(1)} %collective-permute-done.13.refs_3_, ...), custom_call_target="tpu_custom_call" | custom-call | tf_op jit(solution)/shard_map/pallas_call | solution.py:428
  (1 shorter events, 0.0 us)
Async XLA Ops:
  3.6 11.1 %collective-permute-start = (bf16[768,128]{1,0:T(8,128)(2,1)}, bf16[768,128]{1,0:T(8,128)(2,1)S(1)}, u32[]{:S(2)}, u32[]{:S(2)}) collective-permute-start(bf16[768,128]{1,0:T(8,128)(2,1)} %get-tuple-element.37), channel_id=1, source_target_pairs={{0,0},{1,4},{2,2},{3,6},{4,1},{5,5},{6,3},{7,7},{8,8},{9,12},{10,1... | collective-permute-start | bytes 589832 | tf_op jit(solution)/shard_map/ppermute | solution.py:322
  5.2 12.2 %collective-permute-start.2 = (bf16[768,128]{1,0:T(8,128)(2,1)}, bf16[768,128]{1,0:T(8,128)(2,1)S(1)}, u32[]{:S(2)}, u32[]{:S(2)}) collective-permute-start(bf16[768,128]{1,0:T(8,128)(2,1)} %get-tuple-element.51), channel_id=1, source_target_pairs={{0,8},{1,12},{2,10},{3,14},{4,9},{5,13},{6,11},{7,15},{8,0},{9,4},... | collective-permute-start | bytes 589832 | tf_op jit(solution)/shard_map/ppermute | solution.py:322
  8.2 9.2 %collective-permute-start.4 = (bf16[512,128]{1,0:T(8,128)(2,1)}, bf16[512,128]{1,0:T(8,128)(2,1)S(1)}, u32[]{:S(2)}, u32[]{:S(2)}) collective-permute-start(bf16[512,128]{1,0:T(8,128)(2,1)} %get-tuple-element.52), channel_id=1, source_target_pairs={{0,16},{1,20},{2,18},{3,22},{4,17},{5,21},{6,19},{7,23},{8,24},{9,... | collective-permute-start | bytes 393224 | tf_op jit(solution)/shard_map/ppermute | solution.py:322
  10.8 11.3 %collective-permute-start.6 = (bf16[512,128]{1,0:T(8,128)(2,1)}, bf16[512,128]{1,0:T(8,128)(2,1)S(1)}, u32[]{:S(2)}, u32[]{:S(2)}) collective-permute-start(bf16[512,128]{1,0:T(8,128)(2,1)} %get-tuple-element.53), channel_id=1, source_target_pairs={{0,24},{1,28},{2,26},{3,30},{4,25},{5,29},{6,27},{7,31},{8,16},{9,... | collective-permute-start | bytes 393224 | tf_op jit(solution)/shard_map/ppermute | solution.py:322
  14.7 8.7 %collective-permute-start.1 = (bf16[768,128]{1,0:T(8,128)(2,1)S(1)}, bf16[768,128]{1,0:T(8,128)(2,1)S(1)}, u32[]{:S(2)}, u32[]{:S(2)}) collective-permute-start(bf16[768,128]{1,0:T(8,128)(2,1)S(1)} %collective-permute-done.rest_0_.rest_8_), channel_id=1, source_target_pairs={{0,1},{1,0},{2,3},{3,2},{4,5},{5,4},{6,7},{7,6},{8,9},{9,8},{10,11... | collective-permute-start | bytes 589832 | tf_op jit(solution)/shard_map/ppermute | solution.py:328
  17.4 6.1 %collective-permute-start.3 = (bf16[768,128]{1,0:T(8,128)(2,1)S(1)}, bf16[768,128]{1,0:T(8,128)(2,1)S(1)}, u32[]{:S(2)}, u32[]{:S(2)}) collective-permute-start(bf16[768,128]{1,0:T(8,128)(2,1)S(1)} %collective-permute-done.2.rest_2_.rest_9_), channel_id=1, source_target_pairs={{0,1},{1,0},{2,3},{3,2},{4,5},{5,4},{6,7},{7,6},{8,9},{9,8},{10,11... | collective-permute-start | bytes 589832 | tf_op jit(solution)/shard_map/ppermute | solution.py:328
  17.4 5.6 %collective-permute-start.5 = (bf16[512,128]{1,0:T(8,128)(2,1)S(1)}, bf16[512,128]{1,0:T(8,128)(2,1)S(1)}, u32[]{:S(2)}, u32[]{:S(2)}) collective-permute-start(bf16[512,128]{1,0:T(8,128)(2,1)S(1)} %collective-permute-done.4.rest_4_), channel_id=1, source_target_pairs={{0,1},{1,0},{2,3},{3,2},{4,5},{5,4},{6,7},{7,6},{8,9},{9,8},{10,11... | collective-permute-start | bytes 393224 | tf_op jit(solution)/shard_map/ppermute | solution.py:328
  22.1 1.3 %collective-permute-start.7 = (bf16[512,128]{1,0:T(8,128)(2,1)S(1)}, bf16[512,128]{1,0:T(8,128)(2,1)S(1)}, u32[]{:S(2)}, u32[]{:S(2)}) collective-permute-start(bf16[512,128]{1,0:T(8,128)(2,1)S(1)} %collective-permute-done.6.rest_6_), channel_id=1, source_target_pairs={{0,1},{1,0},{2,3},{3,2},{4,5},{5,4},{6,7},{7,6},{8,9},{9,8},{10,11... | collective-permute-start | bytes 393224 | tf_op jit(solution)/shard_map/ppermute | solution.py:328
  22.1 1.4 %copy-start.4 = (s32[216]{0:T(256)S(1)}, s32[216]{0:T(256)}, u32[]{:S(2)}) copy-start(s32[216]{0:T(256)} %get-tuple-element.48.first) | copy-start | bytes 2596
  22.1 1.4 %copy-start = (s32[576]{0:T(1024)S(1)}, s32[576]{0:T(1024)}, u32[]{:S(2)}) copy-start(s32[576]{0:T(1024)} %get-tuple-element.46.which) | copy-start | bytes 6916
  22.1 1.4 %copy-start.3 = (s32[216]{0:T(256)S(1)}, s32[216]{0:T(256)}, u32[]{:S(2)}) copy-start(s32[216]{0:T(256)} %get-tuple-element.47.valid) | copy-start | bytes 2596
  22.1 1.4 %copy-start.5 = (s32[2]{0:T(128)S(1)}, s32[2]{0:T(128)}, u32[]{:S(2)}) copy-start(s32[2]{0:T(128)} %get-tuple-element.49.steps) | copy-start | bytes 28
  22.1 1.4 %copy-start.1 = (s32[216]{0:T(256)S(1)}, s32[216]{0:T(256)}, u32[]{:S(2)}) copy-start(s32[216]{0:T(256)} %get-tuple-element.44.who) | copy-start | bytes 2596
  22.2 1.4 %copy-start.2 = (s32[216]{0:T(256)S(1)}, s32[216]{0:T(256)}, u32[]{:S(2)}) copy-start(s32[216]{0:T(256)} %get-tuple-element.45.where) | copy-start | bytes 2596
  22.2 4.4 %copy-start.6 = (bf16[256,1024]{1,0:T(8,128)(2,1)S(1)}, bf16[256,1024]{1,0:T(8,128)(2,1)}, u32[]{:S(2)}) copy-start(bf16[256,1024]{1,0:T(8,128)(2,1)} %param.11) | copy-start | bytes 1572868
  26.6 1.6 %copy-start.8 = (bf16[256,128]{1,0:T(8,128)(2,1)S(1)}, bf16[256,128]{1,0:T(8,128)(2,1)}, u32[]{:S(2)}) copy-start(bf16[256,128]{1,0:T(8,128)(2,1)} %get-tuple-element.60) | copy-start | bytes 196612
  26.6 5.2 %copy-start.7 = (bf16[256,128]{1,0:T(8,128)(2,1)S(1)}, bf16[256,128]{1,0:T(8,128)(2,1)}, u32[]{:S(2)}) copy-start(bf16[256,128]{1,0:T(8,128)(2,1)} %get-tuple-element.61) | copy-start | bytes 196612
  26.7 31.8 %collective-permute-start.18 = (bf16[256,512]{1,0:T(8,128)(2,1)S(1)}, bf16[256,512]{1,0:T(8,128)(2,1)S(1)}, u32[]{:S(2)}, u32[]{:S(2)}) collective-permute-start(bf16[256,512]{1,0:T(8,128)(2,1)S(1)} %get-tuple-element.65), channel_id=1, source_target_pairs={{0,2},{1,3},{2,0},{3,1},{4,6},{5,7},{6,4},{7,5},{8,10},{9,11},{10,... | collective-permute-start | bytes 786440 | tf_op jit(solution)/shard_map/ppermute | solution.py:331
  28.2 6.7 %collective-permute-start.10 = (bf16[256,128]{1,0:T(8,128)(2,1)S(1)}, bf16[256,128]{1,0:T(8,128)(2,1)S(1)}, u32[]{:S(2)}, u32[]{:S(2)}) collective-permute-start(bf16[256,128]{1,0:T(8,128)(2,1)S(1)} %copy-done.8), channel_id=1, source_target_pairs={{0,16},{1,20},{2,18},{3,22},{4,17},{5,21},{6,19},{7,23},{8,24},{9,... | collective-permute-start | bytes 196616 | tf_op jit(solution)/shard_map/ppermute | solution.py:322
  31.8 6.1 %collective-permute-start.11 = (bf16[256,128]{1,0:T(8,128)(2,1)S(1)}, bf16[256,128]{1,0:T(8,128)(2,1)S(1)}, u32[]{:S(2)}, u32[]{:S(2)}) collective-permute-start(bf16[256,128]{1,0:T(8,128)(2,1)S(1)} %copy-done.7), channel_id=1, source_target_pairs={{0,24},{1,28},{2,26},{3,30},{4,25},{5,29},{6,27},{7,31},{8,16},{9,... | collective-permute-start | bytes 196616 | tf_op jit(solution)/shard_map/ppermute | solution.py:322
  41.7 5.5 %collective-permute-start.12 = (bf16[256,128]{1,0:T(8,128)(2,1)S(1)}, bf16[256,128]{1,0:T(8,128)(2,1)S(1)}, u32[]{:S(2)}, u32[]{:S(2)}) collective-permute-start(bf16[256,128]{1,0:T(8,128)(2,1)S(1)} %get-tuple-element.62), channel_id=1, source_target_pairs={{0,16},{1,20},{2,18},{3,22},{4,17},{5,21},{6,19},{7,23},{8,24},{9,... | collective-permute-start | bytes 196616 | tf_op jit(solution)/shard_map/ppermute | solution.py:322
  42.7 8.6 %collective-permute-start.13 = (bf16[256,128]{1,0:T(8,128)(2,1)S(1)}, bf16[256,128]{1,0:T(8,128)(2,1)S(1)}, u32[]{:S(2)}, u32[]{:S(2)}) collective-permute-start(bf16[256,128]{1,0:T(8,128)(2,1)S(1)} %get-tuple-element.63), channel_id=1, source_target_pairs={{0,24},{1,28},{2,26},{3,30},{4,25},{5,29},{6,27},{7,31},{8,16},{9,... | collective-permute-start | bytes 196616 | tf_op jit(solution)/shard_map/ppermute | solution.py:322
  45.6 5.8 %collective-permute-start.8 = (bf16[256,128]{1,0:T(8,128)(2,1)S(1)}, bf16[256,128]{1,0:T(8,128)(2,1)S(1)}, u32[]{:S(2)}, u32[]{:S(2)}) collective-permute-start(bf16[256,128]{1,0:T(8,128)(2,1)S(1)} %get-tuple-element.54), channel_id=1, source_target_pairs={{0,0},{1,4},{2,2},{3,6},{4,1},{5,5},{6,3},{7,7},{8,8},{9,12},{10,1... | collective-permute-start | bytes 196616 | tf_op jit(solution)/shard_map/ppermute | solution.py:322
  46.2 7.2 %collective-permute-start.9 = (bf16[256,128]{1,0:T(8,128)(2,1)S(1)}, bf16[256,128]{1,0:T(8,128)(2,1)S(1)}, u32[]{:S(2)}, u32[]{:S(2)}) collective-permute-start(bf16[256,128]{1,0:T(8,128)(2,1)S(1)} %get-tuple-element.55), channel_id=1, source_target_pairs={{0,8},{1,12},{2,10},{3,14},{4,9},{5,13},{6,11},{7,15},{8,0},{9,4},... | collective-permute-start | bytes 196616 | tf_op jit(solution)/shard_map/ppermute | solution.py:322
  47.2 6.9 %collective-permute-start.16 = (bf16[256,128]{1,0:T(8,128)(2,1)S(1)}, bf16[256,128]{1,0:T(8,128)(2,1)S(1)}, u32[]{:S(2)}, u32[]{:S(2)}) collective-permute-start(bf16[256,128]{1,0:T(8,128)(2,1)S(1)} %collective-permute-done.12.refs_2_), channel_id=1, source_target_pairs={{0,2},{1,3},{2,0},{3,1},{4,6},{5,7},{6,4},{7,5},{8,10},{9,11},{10,... | collective-permute-start | bytes 196616 | tf_op jit(solution)/shard_map/ppermute | solution.py:331
  51.4 5.0 %collective-permute-start.17 = (bf16[256,128]{1,0:T(8,128)(2,1)S(1)}, bf16[256,128]{1,0:T(8,128)(2,1)S(1)}, u32[]{:S(2)}, u32[]{:S(2)}) collective-permute-start(bf16[256,128]{1,0:T(8,128)(2,1)S(1)} %collective-permute-done.13.refs_3_), channel_id=1, source_target_pairs={{0,2},{1,3},{2,0},{3,1},{4,6},{5,7},{6,4},{7,5},{8,10},{9,11},{10,... | collective-permute-start | bytes 196616 | tf_op jit(solution)/shard_map/ppermute | solution.py:331
  51.4 5.7 %collective-permute-start.14 = (bf16[256,128]{1,0:T(8,128)(2,1)S(1)}, bf16[256,128]{1,0:T(8,128)(2,1)S(1)}, u32[]{:S(2)}, u32[]{:S(2)}) collective-permute-start(bf16[256,128]{1,0:T(8,128)(2,1)S(1)} %collective-permute-done.8.refs_0_), channel_id=1, source_target_pairs={{0,2},{1,3},{2,0},{3,1},{4,6},{5,7},{6,4},{7,5},{8,10},{9,11},{10,... | collective-permute-start | bytes 196616 | tf_op jit(solution)/shard_map/ppermute | solution.py:331
  53.4 5.1 %collective-permute-start.15 = (bf16[256,128]{1,0:T(8,128)(2,1)S(1)}, bf16[256,128]{1,0:T(8,128)(2,1)S(1)}, u32[]{:S(2)}, u32[]{:S(2)}) collective-permute-start(bf16[256,128]{1,0:T(8,128)(2,1)S(1)} %collective-permute-done.9.refs_1_), channel_id=1, source_target_pairs={{0,2},{1,3},{2,0},{3,1},{4,6},{5,7},{6,4},{7,5},{8,10},{9,11},{10,... | collective-permute-start | bytes 196616 | tf_op jit(solution)/shard_map/ppermute | solution.py:331
  58.9 1.6 %collective-permute-start.19 = (bf16[512,256]{1,0:T(8,128)(2,1)S(1)}, bf16[512,256]{1,0:T(8,128)(2,1)S(1)}, u32[]{:S(2)}, u32[]{:S(2)}) collective-permute-start(bf16[512,256]{1,0:T(8,128)(2,1)S(1)} %shard_map.75), channel_id=1, source_target_pairs={{0,1},{1,0},{2,3},{3,2},{4,5},{5,4},{6,7},{7,6},{8,9},{9,8},{10,11... | collective-permute-start | bytes 786440 | tf_op jit(solution)/shard_map/ppermute | solution.py:331
